TPU v7x, 256 devices: a whole 4x4x8 slice. The times are simulated.
256 devices in a mesh: seq: 32 (over x_lo, z, core), chan: 8 (over x_hi, y).
Axes of the slice: x: 4 (x_hi: 2, x_lo: 2; x = x_hi * 2 + x_lo), y: 4, z: 8, core: 2. Of those that a mesh axis runs over, the one named last changes fastest.
Arguments:
- inputs: bfloat16 [262144, 1024], P('seq', 'chan'), may hold values from -6 to 6
- out_grad: bfloat16 [262144, 1024], P('seq', 'chan'), may hold values from -6 to 6
- kernel: bfloat16 [512, 512, 1024], P('seq', None, 'chan'), may hold values from -4 to 4
- gate_weight: bfloat16 [1024, 1024], P(None, 'chan'), may hold values from -0.1875 to 0.1875
- right_factor: bfloat16 [512, 512], replicated, may hold values from -0.25 to 0.25
- left_factor: bfloat16 [512, 512], replicated, may hold values from -0.25 to 0.25
Outputs:
- input_grad: bfloat16 [262144, 1024], P('seq', 'chan')
- kernel_grad: bfloat16 [512, 512, 1024], P('seq', None, 'chan')
- right_grad: float32 [262144], P(('seq', 'chan'))
- left_grad: float32 [262144], P(('seq', 'chan'))
- gate_weight_grad: float32 [1024, 1024], P(('seq', 'chan'))
All inputs are finite; a program needn't handle non-finite values.
Results may differ from a plain program's by a relative error of at most 0.015.
Values may be sent and summed in bfloat16 or wider, within the bound.
No kernel may reach another device: no remote copies, remote signals or barrier semaphores. Data moves between devices by JAX's collectives and lax.ppermute only.
A program may use at most 128 MiB of HBM per device.

v0:
```python
import functools

import jax
import jax.numpy as jnp
from jax import lax
from jax.experimental import pallas as pl
from jax.experimental.pallas import tpu as pltpu
from jax.sharding import PartitionSpec as P


F32 = jnp.float32
BF16 = jnp.bfloat16
NT = (((1,), (1,)), ((), ()))


def call(body, grid, in_specs, out_specs, out_shape, scratch, flops, nbytes):
    return pl.pallas_call(
        body,
        grid_spec=pltpu.PrefetchScalarGridSpec(
            num_scalar_prefetch=1,
            grid=grid,
            in_specs=in_specs,
            out_specs=out_specs,
            scratch_shapes=scratch,
        ),
        out_shape=out_shape,
        cost_estimate=pl.CostEstimate(flops=flops, bytes_accessed=nbytes, transcendentals=0),
    )


def lanes(parts):
    return jnp.concatenate(parts, axis=1)


def first_body(me, x_ref, k_ref, r_ref, tie, u_ref, v_ref, scr, *, step):
    g = pl.program_id(0)
    heads, block = scr.shape[0] // r_ref.shape[0], r_ref.shape[0]
    rhs = lanes([x_ref[t] for t in range(step)])
    prod = jnp.dot(r_ref[...], rhs, preferred_element_type=F32).astype(BF16)
    for t in range(step):
        u = prod[:, t * 128 : (t + 1) * 128]
        u_ref[t] = u
        v = (u.astype(F32) * k_ref[t].astype(F32)).astype(BF16)
        scr[pl.ds(g * step + t, block, stride=heads), :] = v.astype(F32)

    @pl.when(g == pl.num_programs(0) - 1)
    def _():
        def put(s, carry):
            rows = scr[pl.ds(pl.multiple_of(s * heads * heads, 256), heads * heads), :]
            v_ref[s] = rows.reshape(heads, heads, 128).astype(BF16)
            return carry

        lax.fori_loop(0, v_ref.shape[0], put, 0)


def mix_body(me, p_ref, og_ref, l_ref, *outs):
    t = pl.program_id(0)
    block = l_ref.shape[0]
    rhs = lanes([p_ref[:, u].reshape(block, 128) for u in range(2)])
    mixed = jnp.dot(l_ref[...], rhs, preferred_element_type=F32).astype(BF16).astype(F32)
    both = jnp.concatenate(
        [(og_ref[u].astype(F32) * mixed[:, u * 128 : (u + 1) * 128]).astype(BF16) for u in range(2)],
        axis=0,
    )
    for q in range(len(outs)):

        @pl.when(t == q)
        def _(q=q):
            outs[q][...] = both


def gate_body(me, x_ref, w_ref, mine_ref, peer_ref, *refs, n):
    gs, wcat, scr = refs[:n], refs[n], refs[n + 1]

    @pl.when(pl.program_id(0) == 0)
    def _():
        half = w_ref.shape[0] // 2
        near = pl.ds(pl.multiple_of(me[1] * half, half), half)
        far = pl.ds(pl.multiple_of((1 - me[1]) * half, half), half)
        scr[:, :128] = w_ref[...]
        for q in range(1, n):
            scr[near, q * 128 : (q + 1) * 128] = mine_ref[q - 1]
            scr[far, q * 128 : (q + 1) * 128] = peer_ref[q - 1]
        wcat[...] = scr[...]

    rows_in = lanes([x_ref[r] for r in range(n)])
    pre = jnp.dot(rows_in, scr[...], preferred_element_type=F32)
    gate = jax.nn.sigmoid(pre).astype(BF16)
    for q in range(n):
        gs[q][...] = gate[:, q * 128 : (q + 1) * 128]


def turn_body(me, x_ref, out, *, n, seqs):
    g = pl.program_id(0)
    rows, width = out.shape[0], n * 128
    rho = lax.broadcasted_iota(jnp.int32, (rows, width), 0) + g * rows
    col = lax.broadcasted_iota(jnp.int32, (rows, width), 1)
    per = width // (2 * n)
    high = seqs // 2
    own = per // high
    core = me[1] ^ (rho // (width // 2))
    rest = lax.rem(rho, width // 2)
    inner = lax.rem(rest, per)
    seq = lax.rem(inner, high) * 2 + core
    want = (seq * n + (me[0] ^ (rest // per))) * own + inner // high
    pick = jnp.where(want == col, 1.0, 0.0).astype(BF16)
    rows_in = lanes([x_ref[r] for r in range(n)])
    out[...] = lax.dot_general(pick, rows_in, NT, preferred_element_type=F32).astype(BF16)


def back_gate_body(me, *refs, n):
    os, gs, wcat, tie, h_ref, gp_ref = refs[:n], refs[n : 2 * n], *refs[2 * n :]
    parts = []
    for q in range(n):
        g = gs[q][...].astype(F32)
        parts.append((os[q][...].astype(F32) * g * (1.0 - g)).astype(BF16))
    gp = lanes(parts)
    gp_ref[...] = gp
    h = lax.dot_general(gp, wcat[...], NT, preferred_element_type=F32).astype(BF16)
    for d in range(n):
        h_ref[d] = h[:, d * 128 : (d + 1) * 128]


def weight_body(me, xt_ref, gp_ref, mine, peer, *, n):
    g = pl.program_id(0)
    w = jnp.dot(xt_ref[...], gp_ref[...], preferred_element_type=F32).astype(BF16)

    def put(out):
        for q in range(n):
            cols = pl.ds(pl.multiple_of((me[0] ^ q) * 128, 128), 128)
            out[:, cols] = w[:, q * 128 : (q + 1) * 128]

    @pl.when(g < 2)
    def _():
        put(mine)

    @pl.when(g >= 2)
    def _():
        put(peer)


def add_body(me, a_ref, b_ref, right_ref, left_ref, *outs):
    ways = len(outs)
    n, seqs = right_ref.shape[0], right_ref.shape[1]
    per = a_ref.shape[0] // n
    size = per + 2 * seqs
    for r in range(n):
        out, base = outs[r % ways], (r // ways) * size
        rows = slice(r * per, (r + 1) * per)
        both = a_ref[rows, :].astype(F32) + b_ref[rows, :].astype(F32)
        out[base : base + per, :] = both.astype(BF16)
        out[base + per : base + per + seqs, :] = right_ref[r]
        out[base + per + seqs : base + size, :] = left_ref[r]


def mid_body(me, *refs):
    parts, keep, send = refs[:-2], refs[-2], refs[-1]
    size = keep.shape[0]
    keep[...] = total([p[:size, :] for p in parts])
    send[...] = total([p[size:, :] for p in parts]).astype(BF16)


def row_order(me, block, n, seqs):
    rho = lax.broadcasted_iota(jnp.int32, (block, block), 0)
    col = lax.broadcasted_iota(jnp.int32, (block, block), 1)
    per = block // n
    own = per // seqs
    inner = lax.rem(rho, per)
    want = (lax.rem(inner, seqs) * n + (me[0] ^ (rho // per))) * own + inner // seqs
    return jnp.where(want == col, 1.0, 0.0).astype(BF16)


def put_rows(me, acc, n, seqs, put):
    block = acc.shape[0]
    sums = jnp.dot(
        row_order(me, block, n, seqs), acc[...].astype(BF16), preferred_element_type=F32
    ).astype(BF16)
    per = block // n
    for r in range(n):
        for t in range(per // seqs):
            for m in range(block // 128):
                slot = t * (block // 128) + m
                low = r * per + t * seqs
                put(r, slot * 128, sums[low : low + seqs, m * 128 : (m + 1) * 128])


def gate_pick(t, gs, gsc):
    for q in range(len(gs)):

        @pl.when(t == q)
        def _(q=q):
            gsc[...] = gs[q][...]


def grad_mixed_of(og_ref, gsc, block):
    return lanes(
        [
            (og_ref[u].astype(F32) * gsc[u * block : (u + 1) * block, :].astype(F32)).astype(BF16)
            for u in range(2)
        ]
    )


def cot_body(me, *refs, n):
    gs, og_ref, lt_ref, gv_ref, gm_ref, gsc = refs[:n], *refs[n:]
    block = lt_ref.shape[0]
    gate_pick(pl.program_id(0), gs, gsc)
    gm = grad_mixed_of(og_ref, gsc, block)
    gm_ref[...] = gm
    gv = jnp.dot(lt_ref[...], gm, preferred_element_type=F32).astype(BF16)
    for u in range(2):
        gv_ref[:, u] = gv[:, u * 128 : (u + 1) * 128].reshape(gv_ref.shape[0], gv_ref.shape[2], 128)


def accumulate(acc, t, add):
    @pl.when(t == 0)
    def _():
        acc[...] = add

    @pl.when(t > 0)
    def _():
        acc[...] += add


def left_body(me, gm_ref, p_ref, tie, out, acc, *, n, seqs):
    t = pl.program_id(0)
    block = acc.shape[0]
    pairs = gm_ref.shape[0]
    gm = lanes([gm_ref[v] for v in range(pairs)])
    piece = lanes([p_ref[:, u].reshape(block, 128) for u in range(2 * pairs)])
    accumulate(acc, t, lax.dot_general(gm, piece, NT, preferred_element_type=F32))

    @pl.when(t == pl.num_programs(0) - 1)
    def _():
        def put(r, low, value):
            out[r, :, low : low + 128] = value

        put_rows(me, acc, n, seqs, put)


def kernel_grad_body(me, d_ref, u_ref, k_ref, x_ref, kg_ref, gu_ref, out, scr, acc, *, heads, n, seqs):
    t = pl.program_id(0)
    step, block = u_ref.shape[0], u_ref.shape[1]

    @pl.when(t == 0)
    def _():
        def get(s, carry):
            rows = d_ref[s].astype(F32).reshape(heads * heads, 128)
            scr[pl.ds(pl.multiple_of(s * heads * heads, 256), heads * heads), :] = rows
            return carry

        lax.fori_loop(0, d_ref.shape[0], get, 0)

    gus = []
    for u in range(step):
        gv = scr[pl.ds(t * step + u, block, stride=heads), :]
        kg_ref[u] = (gv * u_ref[u].astype(F32)).astype(BF16)
        gu = (gv * k_ref[u].astype(F32)).astype(BF16)
        gu_ref[u] = gu
        gus.append(gu)
    accumulate(
        acc,
        t,
        lax.dot_general(
            lanes(gus), lanes([x_ref[u] for u in range(step)]), NT, preferred_element_type=F32
        ),
    )

    @pl.when(t == pl.num_programs(0) - 1)
    def _():
        def put(r, low, value):
            out[r, :, low : low + 128] = value

        put_rows(me, acc, n, seqs, put)


def input_grad_body(me, h_ref, gu_ref, rt_ref, out):
    block = rt_ref.shape[0]
    rhs = lanes([gu_ref[u] for u in range(2)])
    back = jnp.dot(rt_ref[...], rhs, preferred_element_type=F32)
    for u in range(2):
        rows = slice(u * block, (u + 1) * block)
        out[rows, :] = (back[:, u * 128 : (u + 1) * 128] + h_ref[rows, :].astype(F32)).astype(BF16)


def total(parts):
    return functools.reduce(lambda a, b: a + b, [p.astype(F32) for p in parts])


def pack_body(me, keep, got, out, scr, *, seqs, per):
    slots = out.shape[1]
    sums = keep[...] + got[...].astype(F32)
    weight, right, left = sums[:per], sums[per : per + seqs], sums[per + seqs :]
    blocks = sums.shape[1] // 128
    for slot in range(blocks):
        cols = slice(slot * 128, (slot + 1) * 128)
        scr[pl.ds(slot, seqs, stride=slots), :] = left[:, cols]
        scr[pl.ds(blocks + slot, seqs, stride=slots), :] = right[:, cols]
    high = seqs // 2
    zero = jnp.zeros((high, 128), F32)
    for t in range(per // high):
        for m in range(blocks):
            slot = 2 * blocks + t * blocks + m
            value = weight[t * high : (t + 1) * high, m * 128 : (m + 1) * 128]
            scr[pl.ds(slot + me[1] * slots, high, stride=2 * slots), :] = value
            scr[pl.ds(slot + (1 - me[1]) * slots, high, stride=2 * slots), :] = zero

    def emit(s, carry):
        out[s] = scr[pl.ds(pl.multiple_of(s * slots, 16), slots), :].astype(BF16)
        return carry

    lax.fori_loop(0, seqs, emit, 0)


def share_body(me, p_ref, left_ref, right_ref, weight_ref, *, factor, token):
    sums = lax.fori_loop(
        1, p_ref.shape[0], lambda s, acc: acc + p_ref[s].astype(F32), p_ref[0].astype(F32)
    )
    count = left_ref.shape[0]
    left_ref[...] = sums[:count] * factor
    right_ref[...] = sums[count : 2 * count] * factor
    weight_ref[...] = sums[2 * count :] * token


def local(inputs, out_grad, kernel, gate_weight, right_factor, left_factor):
    block = right_factor.shape[0]
    rows, width = inputs.shape
    model_width = gate_weight.shape[0]
    heads = rows // block
    seqs = block // heads
    n = model_width // width
    part = rows // n
    chan = lax.axis_index("chan")
    core = lax.axis_index("seq") % 2
    pre = jnp.stack([chan, core]).astype(jnp.int32)
    S = jax.ShapeDtypeStruct

    def swap(r, x):
        return x if r == 0 else lax.ppermute(x, "chan", [(i, i ^ r) for i in range(n)])

    def swaps(parts):
        return [swap(r, parts[r]) for r in range(n)]

    def across(x):
        return lax.ppermute(x, "seq", [(i, i ^ 1) for i in range(seqs)])

    def whole(*shape):
        return pl.BlockSpec(shape, lambda t, me: (0,) * len(shape))

    tie = pl.BlockSpec(memory_space=pl.ANY)
    mm = 2 * rows * block * width
    gg = 2 * part * model_width * model_width
    cube = rows * width * 2

    xs = lax.all_to_all(
        inputs.reshape(n, part, width), "chan", split_axis=0, concat_axis=0, tiled=True
    )
    half = lax.dynamic_slice_in_dim(gate_weight, core * (model_width // 2), model_width // 2, 0)
    near = jnp.stack([swap(r, half) for r in range(1, n)])
    far = across(near)

    x_cube = inputs.reshape(heads, block, width)
    og_cube = out_grad.reshape(heads, block, width)
    step = 4
    four = pl.BlockSpec((step, block, width), lambda g, me: (g, 0, 0))
    first, scaled = call(
        functools.partial(first_body, step=step), (heads // step,),
        [four, four, whole(block, block), tie],
        [four, whole(seqs, heads, heads, width)],
        [S((heads, block, width), BF16), S((seqs, heads, heads, width), BF16)],
        [pltpu.VMEM((block * heads, width), F32)],
        mm, 4 * cube,
    )(pre, x_cube, kernel, right_factor, far)
    piece = lax.all_to_all(scaled, "seq", split_axis=0, concat_axis=0, tiled=True)

    chunk = part // 4
    tok = pl.BlockSpec((chunk, width), lambda t, me: (t, 0))
    gate_out = call(
        functools.partial(gate_body, n=n), (part // chunk,),
        [
            pl.BlockSpec((n, chunk, width), lambda t, me: (0, t, 0)),
            whole(model_width, width),
            whole(n - 1, model_width // 2, width),
            whole(n - 1, model_width // 2, width),
        ],
        [tok] * n + [whole(model_width, model_width)],
        [S((part, width), BF16)] * n + [S((model_width, model_width), BF16)],
        [pltpu.VMEM((model_width, model_width), BF16)],
        gg, 4 * cube,
    )(pre, xs, gate_weight, near, far)
    gates_tok, wcat = gate_out[:n], gate_out[n]
    gates = swaps(gates_tok)

    pair_in = pl.BlockSpec((seqs, 2, heads, width), lambda t, me: (0, me[0] ^ t, 0, 0))
    pair_cube = pl.BlockSpec((2, block, width), lambda t, me: (me[0] ^ t, 0, 0))
    grad_mid, grad_mixed = call(
        functools.partial(cot_body, n=n), (n,),
        [whole(part, width)] * n + [pair_cube, whole(block, block)],
        [pair_in, pl.BlockSpec((None, block, 2 * width), lambda t, me: (me[0] ^ t, 0, 0))],
        [S((seqs, heads, heads, width), BF16), S((n, block, 2 * width), BF16)],
        [pltpu.VMEM((part, width), BF16)],
        mm, 4 * cube,
    )(pre, *gates, og_cube, left_factor.T)
    grad_back = lax.all_to_all(grad_mid, "seq", split_axis=0, concat_axis=0, tiled=True)

    om = call(
        mix_body, (n,),
        [pair_in, pair_cube, whole(block, block)],
        [whole(part, width)] * n,
        [S((part, width), BF16)] * n,
        [],
        mm, 3 * cube,
    )(pre, piece, og_cube, left_factor)
    oms = swaps(om)

    count = block * block // (n * seqs * 128)
    lefts = call(
        functools.partial(left_body, n=n, seqs=seqs), (n // 2,),
        [
            pl.BlockSpec((2, block, 2 * width), lambda t, me: (t, 0, 0)),
            pl.BlockSpec((seqs, 4, heads, width), lambda t, me: (0, t, 0, 0)),
            tie,
        ],
        whole(n, seqs, count * 128),
        S((n, seqs, count * 128), BF16),
        [pltpu.VMEM((block, block), F32)],
        mm, 2 * cube,
    )(pre, grad_mixed, piece, om[0])

    turned = call(
        functools.partial(turn_body, n=n, seqs=seqs), (4,),
        [whole(n, part, width)],
        pl.BlockSpec((model_width // 4, part), lambda t, me: (t, 0)),
        S((model_width, part), BF16),
        [],
        gg, 2 * cube,
    )(pre, xs)

    back_gate, grad_pre = call(
        functools.partial(back_gate_body, n=n), (part // chunk,),
        [tok] * n + [tok] * n + [whole(model_width, model_width), tie],
        [
            pl.BlockSpec((n, chunk, width), lambda t, me: (0, t, 0)),
            pl.BlockSpec((chunk, model_width), lambda t, me: (t, 0)),
        ],
        [S((n, part, width), BF16), S((part, model_width), BF16)],
        [],
        gg, 5 * cube,
    )(pre, *oms, *gates_tok, wcat, lefts)
    gate_in = lax.all_to_all(back_gate, "chan", split_axis=0, concat_axis=0, tiled=True)

    quarter = (model_width // 4, model_width)
    mine, other = call(
        functools.partial(weight_body, n=n), (4,),
        [
            pl.BlockSpec((model_width // 4, part), lambda t, me: (t, 0)),
            whole(part, model_width),
        ],
        [
            pl.BlockSpec(quarter, lambda t, me: (jnp.minimum(t, 1), 0)),
            pl.BlockSpec(quarter, lambda t, me: (jnp.maximum(t - 2, 0), 0)),
        ],
        [S((model_width // 2, model_width), BF16)] * 2,
        [],
        gg, 3 * cube,
    )(pre, turned, grad_pre)
    kernel_grad, grad_first, rights = call(
        functools.partial(kernel_grad_body, heads=heads, n=n, seqs=seqs), (heads // step,),
        [whole(seqs, heads, heads, width), four, four, four],
        [four, four, whole(n, seqs, count * 128)],
        [S((heads, block, width), BF16)] * 2 + [S((n, seqs, count * 128), BF16)],
        [pltpu.VMEM((block * heads, width), F32), pltpu.VMEM((block, block), F32)],
        mm, 6 * cube,
    )(pre, grad_back, first, kernel, x_cube)

    ways = n // 2
    per = model_width // (2 * n)
    size = per + 2 * seqs
    pieces = call(
        add_body, (1,),
        [whole(model_width // 2, model_width)] * 2 + [whole(n, seqs, count * 128)] * 2,
        [whole(2 * size, model_width)] * ways,
        [S((2 * size, model_width), BF16)] * ways,
        [],
        cube, 3 * cube,
    )(pre, mine, across(other), rights, lefts)
    keep, send = call(
        mid_body, (1,),
        [whole(2 * size, model_width)] * ways,
        [whole(size, model_width)] * 2,
        [S((size, model_width), F32), S((size, model_width), BF16)],
        [],
        cube, 2 * cube,
    )(pre, *[swap(r, pieces[r]) for r in range(ways)])

    slots = 2 * count + model_width * model_width // (n * seqs * 128)
    packed = call(
        functools.partial(pack_body, seqs=seqs, per=per), (1,),
        [whole(size, model_width)] * 2,
        whole(seqs, slots, 128),
        S((seqs, slots, 128), BF16),
        [pltpu.VMEM((seqs * slots, 128), F32)],
        cube, cube,
    )(pre, keep, swap(ways, send))
    got = lax.all_to_all(packed, "seq", split_axis=0, concat_axis=0, tiled=True)

    input_grad = call(
        input_grad_body, (n,),
        [
            pl.BlockSpec((None, part, width), lambda t, me: (t, 0, 0)),
            pl.BlockSpec((2, block, width), lambda t, me: (t, 0, 0)),
            whole(block, block),
        ],
        pl.BlockSpec((part, width), lambda t, me: (t, 0)),
        S((rows, width), BF16),
        [],
        mm, 3 * cube,
    )(pre, gate_in, grad_first, right_factor.T)

    left_share, right_share, weight_share = call(
        functools.partial(
            share_body, factor=(block * model_width) ** -0.5, token=1.0 / block
        ), (1,),
        [whole(seqs, slots, 128)],
        [whole(count, 128), whole(count, 128), whole(slots - 2 * count, 128)],
        [S((count, 128), F32), S((count, 128), F32), S((slots - 2 * count, 128), F32)],
        [],
        cube, cube,
    )(pre, got)
    return (
        input_grad,
        kernel_grad,
        right_share.reshape(-1),
        left_share.reshape(-1),
        weight_share.reshape(-1, model_width),
    )


def solution(mesh):
    in_specs = (
        P("seq", "chan"),
        P("seq", "chan"),
        P("seq", None, "chan"),
        P(None, "chan"),
        P(),
        P(),
    )
    out_specs = (
        P("seq", "chan"),
        P("seq", None, "chan"),
        P(("seq", "chan")),
        P(("seq", "chan")),
        P(("seq", "chan"), None),
    )
    return jax.shard_map(
        local, mesh=mesh, in_specs=in_specs, out_specs=out_specs, check_vma=False
    )
```

profile of v0, /device:TPU:2, one launch (start us, length us, event | category | flops | bytes accessed | tf_op | source)
XLA Modules:
  0.0 308.9 jit_solution(3330910631307392742)
XLA Ops:
  9.7 6.9 %all-to-all-start.1 = ((bf16[8,1024,128]{2,1,0:T(8,128)(2,1)}), bf16[8,1024,128]{2,1,0:T(8,128)(2,1)S(1)}, u32[]{:S(2)}, u32[]{:S(2)}) async-start(bf16[8,1024,128]{2,1,0:T(8,128)(2,1)} %bitcast.23), calls=%async_computation.1 | async-start | bytes 4194304 | tf_op jit(solution)/shard_map/all_to_all | solution.py:355
  16.6 5.9 %collective-permute-start.5 = (bf16[512,128]{1,0:T(8,128)(2,1)S(1)}, bf16[512,128]{1,0:T(8,128)(2,1)S(1)}, u32[]{:S(2)}, u32[]{:S(2)}) collective-permute-start(bf16[512,128]{1,0:T(8,128)(2,1)S(1)} %constant_dynamic-slice_fusion), channel_id=1, source_target_pairs={{0,6},{1,7},{2,4},{3,5},{4,2},{5,3},{6,0},{7,1},{8,14},{9,15},{10,... | collective-permute-start | bytes 393224 | tf_op jit(solution)/shard_map/ppermute | solution.py:339
  27.1 21.5 %collective-permute-done.5 = bf16[512,128]{1,0:T(8,128)(2,1)S(1)} collective-permute-done((bf16[512,128]{1,0:T(8,128)(2,1)S(1)}, bf16[512,128]{1,0:T(8,128)(2,1)S(1)}, u32[]{:S(2)}, u32[]{:S(2)}) %collective-permute-start.5) | collective-permute-done | bytes 131104 | tf_op jit(solution)/shard_map/ppermute | solution.py:339
  53.9 7.4 %shard_map.101 = (bf16[16,512,128]{2,1,0:T(8,128)(2,1)}, bf16[32,16,16,128]{3,2,1,0:T(8,128)(2,1)}) custom-call(s32[2]{0:T(128)} %pad_add_fusion.me, bf16[16,512,128]{2,1,0:T(8,128)(2,1)} %bitcast.24, bf16[16,512,128]{2,1,0:T(8,128)(2,1)} %k_ref.3, bf16[512,512]{1,0:T(8,128)(2,1)} %r_ref.1, bf16[7,512,128]{2,1,0:T(8,128)(2,1)} %copy-done.7), custom_call_target="tpu_custom_call" | custom-call | flops 1073741824 | bytes 8388608 | tf_op jit(solution)/shard_map/pallas_call | solution.py:366
  62.7 10.1 %all-to-all-start = ((bf16[32,16,16,128]{3,2,1,0:T(8,128)(2,1)}), bf16[32,16,16,128]{3,2,1,0:T(8,128)(2,1)S(1)}, u32[]{:S(2)}, u32[]{:S(2)}) async-start(bf16[32,16,16,128]{3,2,1,0:T(8,128)(2,1)} %get-tuple-element.42), calls=%async_computation | async-start | bytes 4194304 | tf_op jit(solution)/shard_map/all_to_all | solution.py:374
  72.8 8.0 %shard_map.103 = (bf16[1024,128]{1,0:T(8,128)(2,1)}, bf16[1024,128]{1,0:T(8,128)(2,1)}, bf16[1024,128]{1,0:T(8,128)(2,1)}, bf16[1024,128]{1,0:T(8,128)(2,1)}, bf...) custom-call(s32[2]{0:T(128)} %pad_add_fusion.me, ...), custom_call_target="tpu_custom_call" | custom-call | flops 2147483648 | bytes 8388608 | tf_op jit(solution)/shard_map/pallas_call | solution.py:378
  91.6 4.2 %collective-permute-done.16.refs_2_ = bf16[1024,128]{1,0:T(8,128)(2,1)S(1)} collective-permute-done((bf16[1024,128]{1,0:T(8,128)(2,1)}, bf16[1024,128]{1,0:T(8,128)(2,1)S(1)}, u32[]{:S(2)}, u32[]{:S(2)}) %collective-permute-start.16) | collective-permute-done | bytes 262176 | tf_op jit(solution)/shard_map/ppermute | solution.py:339
  100.6 9.0 %collective-permute-done.19.refs_5_ = bf16[1024,128]{1,0:T(8,128)(2,1)} collective-permute-done((bf16[1024,128]{1,0:T(8,128)(2,1)}, bf16[1024,128]{1,0:T(8,128)(2,1)}, u32[]{:S(2)}, u32[]{:S(2)}) %collective-permute-start.19) | collective-permute-done | bytes 262176 | tf_op jit(solution)/shard_map/ppermute | solution.py:339
  109.6 9.3 %collective-permute-done.20.refs_6_ = bf16[1024,128]{1,0:T(8,128)(2,1)} collective-permute-done((bf16[1024,128]{1,0:T(8,128)(2,1)}, bf16[1024,128]{1,0:T(8,128)(2,1)}, u32[]{:S(2)}, u32[]{:S(2)}) %collective-permute-start.20) | collective-permute-done | bytes 262176 | tf_op jit(solution)/shard_map/ppermute | solution.py:339
  119.0 7.8 %collective-permute-done.21.refs_7_ = bf16[1024,128]{1,0:T(8,128)(2,1)} collective-permute-done((bf16[1024,128]{1,0:T(8,128)(2,1)}, bf16[1024,128]{1,0:T(8,128)(2,1)}, u32[]{:S(2)}, u32[]{:S(2)}) %collective-permute-start.21) | collective-permute-done | bytes 262176 | tf_op jit(solution)/shard_map/ppermute | solution.py:339
  126.8 8.9 %shard_map.104 = (bf16[32,16,16,128]{3,2,1,0:T(8,128)(2,1)}, bf16[8,512,256]{2,1,0:T(8,128)(2,1)}) custom-call(s32[2]{0:T(128)} %pad_add_fusion.me, bf16[1024,128]{1,0:T(8,128)(2,1)} %get-tuple-element.51.refs_0_.refs_8_, bf16[1024,128]{1,0:T(8,128)(2,1)} %copy-done.9, bf16[1024,128]{1,0:T(8,128)(2,1)} %copy-done.10, bf16[1024,128]{1,0:T(8,128)(2,1)} %copy-done.11, ...), custom_call_target="tpu_custom_call" | custom-call | flops 1073741824 | bytes 8388608 | tf_op jit(solution)/shard_map/pallas_call | solution.py:396
  137.1 7.2 %all-to-all-start.3 = ((bf16[32,16,16,128]{3,2,1,0:T(8,128)(2,1)}), bf16[32,16,16,128]{3,2,1,0:T(8,128)(2,1)}, u32[]{:S(2)}, u32[]{:S(2)}) async-start(bf16[32,16,16,128]{3,2,1,0:T(8,128)(2,1)} %get-tuple-element.62), calls=%async_computation.3 | async-start | bytes 4194304 | tf_op jit(solution)/shard_map/all_to_all | solution.py:404
  144.3 8.4 %shard_map.102 = (bf16[1024,128]{1,0:T(8,128)(2,1)}, bf16[1024,128]{1,0:T(8,128)(2,1)}, bf16[1024,128]{1,0:T(8,128)(2,1)}, bf16[1024,128]{1,0:T(8,128)(2,1)}, bf...) custom-call(s32[2]{0:T(128)} %pad_add_fusion.me, ...), custom_call_target="tpu_custom_call" | custom-call | flops 1073741824 | bytes 6291456 | tf_op jit(solution)/shard_map/pallas_call | solution.py:406
  157.3 3.9 %collective-permute-start.13 = (bf16[1024,128]{1,0:T(8,128)(2,1)}, bf16[1024,128]{1,0:T(8,128)(2,1)S(1)}, u32[]{:S(2)}, u32[]{:S(2)}) collective-permute-start(bf16[1024,128]{1,0:T(8,128)(2,1)} %get-tuple-element.49), channel_id=1, source_target_pairs={{0,6},{1,7},{2,4},{3,5},{4,2},{5,3},{6,0},{7,1},{8,14},{9,15},{10,... | collective-permute-start | bytes 786440 | tf_op jit(solution)/shard_map/ppermute | solution.py:339
  161.2 3.3 %collective-permute-start.14 = (bf16[1024,128]{1,0:T(8,128)(2,1)}, bf16[1024,128]{1,0:T(8,128)(2,1)S(1)}, u32[]{:S(2)}, u32[]{:S(2)}) collective-permute-start(bf16[1024,128]{1,0:T(8,128)(2,1)} %get-tuple-element.50), channel_id=1, source_target_pairs={{0,7},{1,6},{2,5},{3,4},{4,3},{5,2},{6,1},{7,0},{8,15},{9,14},{10,... | collective-permute-start | bytes 786440 | tf_op jit(solution)/shard_map/ppermute | solution.py:339
  164.5 4.8 %collective-permute-done.11.refs_4_ = bf16[1024,128]{1,0:T(8,128)(2,1)S(1)} collective-permute-done((bf16[1024,128]{1,0:T(8,128)(2,1)}, bf16[1024,128]{1,0:T(8,128)(2,1)S(1)}, u32[]{:S(2)}, u32[]{:S(2)}) %collective-permute-start.11) | collective-permute-done | bytes 262176 | tf_op jit(solution)/shard_map/ppermute | solution.py:339
  169.9 6.8 %shard_map.109.xt_ref = bf16[1024,1024]{1,0:T(8,128)(2,1)} custom-call(s32[2]{0:T(128)} %pad_add_fusion.me, bf16[8,1024,128]{2,1,0:T(8,128)(2,1)} %copy-done.4), custom_call_target="tpu_custom_call" | custom-call | flops 2147483648 | bytes 4194304 | tf_op jit(solution)/shard_map/pallas_call | solution.py:430
  176.7 6.1 %shard_map.105.refs_17_.left_ref = bf16[8,32,1024]{2,1,0:T(8,128)(2,1)} custom-call(s32[2]{0:T(128)} %pad_add_fusion.me, bf16[8,512,256]{2,1,0:T(8,128)(2,1)} %get-tuple-element.60.gm_ref, bf16[32,16,16,128]{3,2,1,0:T(8,128)(2,1)} %copy-done, bf16[1024,128]{1,0:T(8,128)(2,1)} %get-tuple-element.43.tie.refs_0_), custom_call_target="tpu_custom_call" | custom-call | flops 1073741824 | bytes 4194304 | tf_op jit(solution)/shard_map/pallas_call | solution.py:417
  182.8 7.0 %collective-permute-done.13.refs_6_ = bf16[1024,128]{1,0:T(8,128)(2,1)S(1)} collective-permute-done((bf16[1024,128]{1,0:T(8,128)(2,1)}, bf16[1024,128]{1,0:T(8,128)(2,1)S(1)}, u32[]{:S(2)}, u32[]{:S(2)}) %collective-permute-start.13) | collective-permute-done | bytes 262176 | tf_op jit(solution)/shard_map/ppermute | solution.py:339
  189.8 7.1 %collective-permute-done.14.refs_7_ = bf16[1024,128]{1,0:T(8,128)(2,1)S(1)} collective-permute-done((bf16[1024,128]{1,0:T(8,128)(2,1)}, bf16[1024,128]{1,0:T(8,128)(2,1)S(1)}, u32[]{:S(2)}, u32[]{:S(2)}) %collective-permute-start.14) | collective-permute-done | bytes 262176 | tf_op jit(solution)/shard_map/ppermute | solution.py:339
  197.8 7.7 %shard_map.106 = (bf16[8,1024,128]{2,1,0:T(8,128)(2,1)}, bf16[1024,1024]{1,0:T(8,128)(2,1)}) custom-call(s32[2]{0:T(128)} %pad_add_fusion.me, bf16[1024,128]{1,0:T(8,128)(2,1)} %get-tuple-element.43.tie.refs_0_, bf16[1024,128]{1,0:T(8,128)(2,1)} %copy-done.18, bf16[1024,128]{1,0:T(8,128)(2,1)} %copy-done.19, bf16[1024,128]{1,0:T(8,128)(2,1)} %copy-done.13, ...), custom_call_target="tpu_custom_call" | custom-call | flops 2147483648 | bytes 10485760 | tf_op jit(solution)/shard_map/pallas_call | solution.py:439
  205.5 7.3 %shard_map.110 = (bf16[512,1024]{1,0:T(8,128)(2,1)}, bf16[512,1024]{1,0:T(8,128)(2,1)}) custom-call(s32[2]{0:T(128)} %pad_add_fusion.me, bf16[1024,1024]{1,0:T(8,128)(2,1)} %shard_map.109.xt_ref, bf16[1024,1024]{1,0:T(8,128)(2,1)} %get-tuple-element.66.gp_ref), custom_call_target="tpu_custom_call" | custom-call | flops 2147483648 | bytes 6291456 | tf_op jit(solution)/shard_map/pallas_call | solution.py:453
  212.8 4.5 %all-to-all-start.2 = ((bf16[8,1024,128]{2,1,0:T(8,128)(2,1)}), bf16[8,1024,128]{2,1,0:T(8,128)(2,1)S(1)}, u32[]{:S(2)}, u32[]{:S(2)}) async-start(bf16[8,1024,128]{2,1,0:T(8,128)(2,1)} %get-tuple-element.61), calls=%async_computation.2 | async-start | bytes 4194304 | tf_op jit(solution)/shard_map/all_to_all | solution.py:450
  217.3 9.2 %shard_map.107 = (bf16[16,512,128]{2,1,0:T(8,128)(2,1)}, bf16[16,512,128]{2,1,0:T(8,128)(2,1)}, bf16[8,32,1024]{2,1,0:T(8,128)(2,1)}) custom-call(s32[2]{0:T(128)} %pad_add_fusion.me, bf16[32,16,16,128]{3,2,1,0:T(8,128)(2,1)} %all-to-all-done.3.d_ref, bf16[16,512,128]{2,1,0:T(8,128)(2,1)} %get-tuple-element.63.u_ref, bf16[16,512,128]{2,1,0:T(8,128)(2,1)} %k_ref.3, ...), custom_call_target="tpu_custom_call" | custom-call | flops 1073741824 | bytes 12582912 | tf_op jit(solution)/shard_map/pallas_call | solution.py:467
  227.4 3.9 %shard_map.111 = (bf16[256,1024]{1,0:T(8,128)(2,1)}, bf16[256,1024]{1,0:T(8,128)(2,1)}, bf16[256,1024]{1,0:T(8,128)(2,1)}, bf16[256,1024]{1,0:T(8,128)(2,1)}) custom-call(s32[2]{0:T(128)} %pad_add_fusion.me, bf16[512,1024]{1,0:T(8,128)(2,1)} %get-tuple-element.67.a_ref, bf16[512,1024]{1,0:T(8,128)(2,1)} %copy-done.6, ...), custom_call_target="tpu_custom_call" | custom-call | flops 2097152 | bytes 6291456 | tf_op jit(solution)/shard_map/pallas_call | solution.py:479
  236.0 18.7 %collective-permute-done.23.refs_1_ = bf16[256,1024]{1,0:T(8,128)(2,1)S(1)} collective-permute-done((bf16[256,1024]{1,0:T(8,128)(2,1)}, bf16[256,1024]{1,0:T(8,128)(2,1)S(1)}, u32[]{:S(2)}, u32[]{:S(2)}) %collective-permute-start.23) | collective-permute-done | bytes 524320 | tf_op jit(solution)/shard_map/ppermute | solution.py:339
  254.8 12.1 %collective-permute-done.24.refs_2_ = bf16[256,1024]{1,0:T(8,128)(2,1)} collective-permute-done((bf16[256,1024]{1,0:T(8,128)(2,1)}, bf16[256,1024]{1,0:T(8,128)(2,1)}, u32[]{:S(2)}, u32[]{:S(2)}) %collective-permute-start.24) | collective-permute-done | bytes 524320 | tf_op jit(solution)/shard_map/ppermute | solution.py:339
  273.0 6.3 %collective-permute-done.26.got = bf16[128,1024]{1,0:T(8,128)(2,1)S(1)} collective-permute-done((bf16[128,1024]{1,0:T(8,128)(2,1)}, bf16[128,1024]{1,0:T(8,128)(2,1)S(1)}, u32[]{:S(2)}, u32[]{:S(2)}) %collective-permute-start.26) | collective-permute-done | bytes 262176 | tf_op jit(solution)/shard_map/ppermute | solution.py:339
  280.1 3.2 %shard_map.113 = bf16[32,48,128]{2,1,0:T(8,128)(2,1)} custom-call(s32[2]{0:T(128)} %pad_add_fusion.me, f32[128,1024]{1,0:T(8,128)} %get-tuple-element.74.keep, bf16[128,1024]{1,0:T(8,128)(2,1)} %copy-done.12), custom_call_target="tpu_custom_call" | custom-call | flops 2097152 | bytes 2097152 | tf_op jit(solution)/shard_map/pallas_call | solution.py:497
  283.3 6.5 %all-to-all-start.4 = ((bf16[32,48,128]{2,1,0:T(8,128)(2,1)}), bf16[32,48,128]{2,1,0:T(8,128)(2,1)S(1)}, u32[]{:S(2)}, u32[]{:S(2)}) async-start(bf16[32,48,128]{2,1,0:T(8,128)(2,1)} %shard_map.113), calls=%async_computation.4 | async-start | bytes 786432 | tf_op jit(solution)/shard_map/all_to_all | solution.py:505
  290.9 7.9 %shard_map.108 = bf16[8192,128]{1,0:T(8,128)(2,1)} custom-call(s32[2]{0:T(128)} %pad_add_fusion.me, bf16[8,1024,128]{2,1,0:T(8,128)(2,1)} %copy-done.1, bf16[16,512,128]{2,1,0:T(8,128)(2,1)} %get-tuple-element.64.gu_ref, bf16[512,512]{1,0:T(8,128)(2,1)} %bitcast.29), custom_call_target="tpu_custom_call" | custom-call | flops 1073741824 | bytes 6291456 | tf_op jit(solution)/shard_map/pallas_call | solution.py:507
  298.8 5.6 %all-to-all-done.4.p_ref = bf16[32,48,128]{2,1,0:T(8,128)(2,1)S(1)} async-done(((bf16[32,48,128]{2,1,0:T(8,128)(2,1)}), bf16[32,48,128]{2,1,0:T(8,128)(2,1)S(1)}, u32[]{:S(2)}, u32[]{:S(2)}) %all-to-all-start.4) | async-done | bytes 393248 | tf_op jit(solution)/shard_map/all_to_all | solution.py:505
  (98 shorter events, 61.6 us)
Async XLA Ops:
  1.6 15.1 %collective-permute-start = (bf16[512,128]{1,0:T(8,128)(2,1)S(1)}, bf16[512,128]{1,0:T(8,128)(2,1)S(1)}, u32[]{:S(2)}, u32[]{:S(2)}) collective-permute-start(bf16[512,128]{1,0:T(8,128)(2,1)S(1)} %constant_dynamic-slice_fusion), channel_id=1, source_target_pairs={{0,1},{1,0},{2,3},{3,2},{4,5},{5,4},{6,7},{7,6},{8,9},{9,8},{10,11... | collective-permute-start | bytes 393224 | tf_op jit(solution)/shard_map/ppermute | solution.py:339
  3.2 20.0 %collective-permute-start.1 = (bf16[512,128]{1,0:T(8,128)(2,1)S(1)}, bf16[512,128]{1,0:T(8,128)(2,1)S(1)}, u32[]{:S(2)}, u32[]{:S(2)}) collective-permute-start(bf16[512,128]{1,0:T(8,128)(2,1)S(1)} %constant_dynamic-slice_fusion), channel_id=1, source_target_pairs={{0,2},{1,3},{2,0},{3,1},{4,6},{5,7},{6,4},{7,5},{8,10},{9,11},{10,... | collective-permute-start | bytes 393224 | tf_op jit(solution)/shard_map/ppermute | solution.py:339
  6.1 18.9 %collective-permute-start.2 = (bf16[512,128]{1,0:T(8,128)(2,1)S(1)}, bf16[512,128]{1,0:T(8,128)(2,1)S(1)}, u32[]{:S(2)}, u32[]{:S(2)}) collective-permute-start(bf16[512,128]{1,0:T(8,128)(2,1)S(1)} %constant_dynamic-slice_fusion), channel_id=1, source_target_pairs={{0,3},{1,2},{2,1},{3,0},{4,7},{5,6},{6,5},{7,4},{8,11},{9,10},{10,... | collective-permute-start | bytes 393224 | tf_op jit(solution)/shard_map/ppermute | solution.py:339
  6.4 19.4 %collective-permute-start.3 = (bf16[512,128]{1,0:T(8,128)(2,1)S(1)}, bf16[512,128]{1,0:T(8,128)(2,1)S(1)}, u32[]{:S(2)}, u32[]{:S(2)}) collective-permute-start(bf16[512,128]{1,0:T(8,128)(2,1)S(1)} %constant_dynamic-slice_fusion), channel_id=1, source_target_pairs={{0,4},{1,5},{2,6},{3,7},{4,0},{5,1},{6,2},{7,3},{8,12},{9,13},{10,... | collective-permute-start | bytes 393224 | tf_op jit(solution)/shard_map/ppermute | solution.py:339
  8.5 17.9 %collective-permute-start.4 = (bf16[512,128]{1,0:T(8,128)(2,1)S(1)}, bf16[512,128]{1,0:T(8,128)(2,1)S(1)}, u32[]{:S(2)}, u32[]{:S(2)}) collective-permute-start(bf16[512,128]{1,0:T(8,128)(2,1)S(1)} %constant_dynamic-slice_fusion), channel_id=1, source_target_pairs={{0,5},{1,4},{2,7},{3,6},{4,1},{5,0},{6,3},{7,2},{8,13},{9,12},{10,... | collective-permute-start | bytes 393224 | tf_op jit(solution)/shard_map/ppermute | solution.py:339
  9.7 51.6 %all-to-all-start.1 = ((bf16[8,1024,128]{2,1,0:T(8,128)(2,1)}), bf16[8,1024,128]{2,1,0:T(8,128)(2,1)S(1)}, u32[]{:S(2)}, u32[]{:S(2)}) async-start(bf16[8,1024,128]{2,1,0:T(8,128)(2,1)} %bitcast.23), calls=%async_computation.1 | async-start | bytes 4194304 | tf_op jit(solution)/shard_map/all_to_all | solution.py:355
  16.6 31.9 %collective-permute-start.5 = (bf16[512,128]{1,0:T(8,128)(2,1)S(1)}, bf16[512,128]{1,0:T(8,128)(2,1)S(1)}, u32[]{:S(2)}, u32[]{:S(2)}) collective-permute-start(bf16[512,128]{1,0:T(8,128)(2,1)S(1)} %constant_dynamic-slice_fusion), channel_id=1, source_target_pairs={{0,6},{1,7},{2,4},{3,5},{4,2},{5,3},{6,0},{7,1},{8,14},{9,15},{10,... | collective-permute-start | bytes 393224 | tf_op jit(solution)/shard_map/ppermute | solution.py:339
  23.2 26.4 %collective-permute-start.6 = (bf16[512,128]{1,0:T(8,128)(2,1)S(1)}, bf16[512,128]{1,0:T(8,128)(2,1)S(1)}, u32[]{:S(2)}, u32[]{:S(2)}) collective-permute-start(bf16[512,128]{1,0:T(8,128)(2,1)S(1)} %constant_dynamic-slice_fusion), channel_id=1, source_target_pairs={{0,7},{1,6},{2,5},{3,4},{4,3},{5,2},{6,1},{7,0},{8,15},{9,14},{10,... | collective-permute-start | bytes 393224 | tf_op jit(solution)/shard_map/ppermute | solution.py:339
  50.3 2.7 collective-permute-start.7
  62.7 73.1 %all-to-all-start = ((bf16[32,16,16,128]{3,2,1,0:T(8,128)(2,1)}), bf16[32,16,16,128]{3,2,1,0:T(8,128)(2,1)S(1)}, u32[]{:S(2)}, u32[]{:S(2)}) async-start(bf16[32,16,16,128]{3,2,1,0:T(8,128)(2,1)} %get-tuple-element.42), calls=%async_computation | async-start | bytes 4194304 | tf_op jit(solution)/shard_map/all_to_all | solution.py:374
  80.7 9.5 %collective-permute-start.15 = (bf16[1024,128]{1,0:T(8,128)(2,1)}, bf16[1024,128]{1,0:T(8,128)(2,1)S(1)}, u32[]{:S(2)}, u32[]{:S(2)}) collective-permute-start(bf16[1024,128]{1,0:T(8,128)(2,1)} %get-tuple-element.52.refs_9_), channel_id=1, source_target_pairs={{0,1},{1,0},{2,3},{3,2},{4,5},{5,4},{6,7},{7,6},{8,9},{9,8},{10,11... | collective-permute-start | bytes 786440 | tf_op jit(solution)/shard_map/ppermute | solution.py:339
  81.4 14.5 %collective-permute-start.16 = (bf16[1024,128]{1,0:T(8,128)(2,1)}, bf16[1024,128]{1,0:T(8,128)(2,1)S(1)}, u32[]{:S(2)}, u32[]{:S(2)}) collective-permute-start(bf16[1024,128]{1,0:T(8,128)(2,1)} %get-tuple-element.53.refs_10_), channel_id=1, source_target_pairs={{0,2},{1,3},{2,0},{3,1},{4,6},{5,7},{6,4},{7,5},{8,10},{9,11},{10,... | collective-permute-start | bytes 786440 | tf_op jit(solution)/shard_map/ppermute | solution.py:339
  83.6 15.1 %collective-permute-start.17 = (bf16[1024,128]{1,0:T(8,128)(2,1)}, bf16[1024,128]{1,0:T(8,128)(2,1)S(1)}, u32[]{:S(2)}, u32[]{:S(2)}) collective-permute-start(bf16[1024,128]{1,0:T(8,128)(2,1)} %get-tuple-element.54.refs_11_), channel_id=1, source_target_pairs={{0,3},{1,2},{2,1},{3,0},{4,7},{5,6},{6,5},{7,4},{8,11},{9,10},{10,... | collective-permute-start | bytes 786440 | tf_op jit(solution)/shard_map/ppermute | solution.py:339
  85.5 15.1 %collective-permute-start.18 = (bf16[1024,128]{1,0:T(8,128)(2,1)}, bf16[1024,128]{1,0:T(8,128)(2,1)}, u32[]{:S(2)}, u32[]{:S(2)}) collective-permute-start(bf16[1024,128]{1,0:T(8,128)(2,1)} %get-tuple-element.55.refs_12_), channel_id=1, source_target_pairs={{0,4},{1,5},{2,6},{3,7},{4,0},{5,1},{6,2},{7,3},{8,12},{9,13},{10,... | collective-permute-start | bytes 786440 | tf_op jit(solution)/shard_map/ppermute | solution.py:339
  86.0 23.6 %collective-permute-start.19 = (bf16[1024,128]{1,0:T(8,128)(2,1)}, bf16[1024,128]{1,0:T(8,128)(2,1)}, u32[]{:S(2)}, u32[]{:S(2)}) collective-permute-start(bf16[1024,128]{1,0:T(8,128)(2,1)} %get-tuple-element.56.refs_13_), channel_id=1, source_target_pairs={{0,5},{1,4},{2,7},{3,6},{4,1},{5,0},{6,3},{7,2},{8,13},{9,12},{10,... | collective-permute-start | bytes 786440 | tf_op jit(solution)/shard_map/ppermute | solution.py:339
  90.2 28.8 %collective-permute-start.20 = (bf16[1024,128]{1,0:T(8,128)(2,1)}, bf16[1024,128]{1,0:T(8,128)(2,1)}, u32[]{:S(2)}, u32[]{:S(2)}) collective-permute-start(bf16[1024,128]{1,0:T(8,128)(2,1)} %get-tuple-element.57.refs_14_), channel_id=1, source_target_pairs={{0,6},{1,7},{2,4},{3,5},{4,2},{5,3},{6,0},{7,1},{8,14},{9,15},{10,... | collective-permute-start | bytes 786440 | tf_op jit(solution)/shard_map/ppermute | solution.py:339
  95.8 30.9 %collective-permute-start.21 = (bf16[1024,128]{1,0:T(8,128)(2,1)}, bf16[1024,128]{1,0:T(8,128)(2,1)}, u32[]{:S(2)}, u32[]{:S(2)}) collective-permute-start(bf16[1024,128]{1,0:T(8,128)(2,1)} %get-tuple-element.58.refs_15_), channel_id=1, source_target_pairs={{0,7},{1,6},{2,5},{3,4},{4,3},{5,2},{6,1},{7,0},{8,15},{9,14},{10,... | collective-permute-start | bytes 786440 | tf_op jit(solution)/shard_map/ppermute | solution.py:339
  137.1 75.7 %all-to-all-start.3 = ((bf16[32,16,16,128]{3,2,1,0:T(8,128)(2,1)}), bf16[32,16,16,128]{3,2,1,0:T(8,128)(2,1)}, u32[]{:S(2)}, u32[]{:S(2)}) async-start(bf16[32,16,16,128]{3,2,1,0:T(8,128)(2,1)} %get-tuple-element.62), calls=%async_computation.3 | async-start | bytes 4194304 | tf_op jit(solution)/shard_map/all_to_all | solution.py:404
  152.7 11.8 %collective-permute-start.10 = (bf16[1024,128]{1,0:T(8,128)(2,1)}, bf16[1024,128]{1,0:T(8,128)(2,1)S(1)}, u32[]{:S(2)}, u32[]{:S(2)}) collective-permute-start(bf16[1024,128]{1,0:T(8,128)(2,1)} %get-tuple-element.46), channel_id=1, source_target_pairs={{0,3},{1,2},{2,1},{3,0},{4,7},{5,6},{6,5},{7,4},{8,11},{9,10},{10,... | collective-permute-start | bytes 786440 | tf_op jit(solution)/shard_map/ppermute | solution.py:339
  154.4 14.9 %collective-permute-start.11 = (bf16[1024,128]{1,0:T(8,128)(2,1)}, bf16[1024,128]{1,0:T(8,128)(2,1)S(1)}, u32[]{:S(2)}, u32[]{:S(2)}) collective-permute-start(bf16[1024,128]{1,0:T(8,128)(2,1)} %get-tuple-element.47), channel_id=1, source_target_pairs={{0,4},{1,5},{2,6},{3,7},{4,0},{5,1},{6,2},{7,3},{8,12},{9,13},{10,... | collective-permute-start | bytes 786440 | tf_op jit(solution)/shard_map/ppermute | solution.py:339
  155.6 27.2 %collective-permute-start.12 = (bf16[1024,128]{1,0:T(8,128)(2,1)}, bf16[1024,128]{1,0:T(8,128)(2,1)S(1)}, u32[]{:S(2)}, u32[]{:S(2)}) collective-permute-start(bf16[1024,128]{1,0:T(8,128)(2,1)} %get-tuple-element.48), channel_id=1, source_target_pairs={{0,5},{1,4},{2,7},{3,6},{4,1},{5,0},{6,3},{7,2},{8,13},{9,12},{10,... | collective-permute-start | bytes 786440 | tf_op jit(solution)/shard_map/ppermute | solution.py:339
  157.3 32.5 %collective-permute-start.13 = (bf16[1024,128]{1,0:T(8,128)(2,1)}, bf16[1024,128]{1,0:T(8,128)(2,1)S(1)}, u32[]{:S(2)}, u32[]{:S(2)}) collective-permute-start(bf16[1024,128]{1,0:T(8,128)(2,1)} %get-tuple-element.49), channel_id=1, source_target_pairs={{0,6},{1,7},{2,4},{3,5},{4,2},{5,3},{6,0},{7,1},{8,14},{9,15},{10,... | collective-permute-start | bytes 786440 | tf_op jit(solution)/shard_map/ppermute | solution.py:339
  161.2 35.7 %collective-permute-start.14 = (bf16[1024,128]{1,0:T(8,128)(2,1)}, bf16[1024,128]{1,0:T(8,128)(2,1)S(1)}, u32[]{:S(2)}, u32[]{:S(2)}) collective-permute-start(bf16[1024,128]{1,0:T(8,128)(2,1)} %get-tuple-element.50), channel_id=1, source_target_pairs={{0,7},{1,6},{2,5},{3,4},{4,3},{5,2},{6,1},{7,0},{8,15},{9,14},{10,... | collective-permute-start | bytes 786440 | tf_op jit(solution)/shard_map/ppermute | solution.py:339
  164.5 32.5 %collective-permute-start.8 = (bf16[1024,128]{1,0:T(8,128)(2,1)}, bf16[1024,128]{1,0:T(8,128)(2,1)S(1)}, u32[]{:S(2)}, u32[]{:S(2)}) collective-permute-start(bf16[1024,128]{1,0:T(8,128)(2,1)} %get-tuple-element.44), channel_id=1, source_target_pairs={{0,1},{1,0},{2,3},{3,2},{4,5},{5,4},{6,7},{7,6},{8,9},{9,8},{10,11... | collective-permute-start | bytes 786440 | tf_op jit(solution)/shard_map/ppermute | solution.py:339
  169.3 27.7 %collective-permute-start.9 = (bf16[1024,128]{1,0:T(8,128)(2,1)}, bf16[1024,128]{1,0:T(8,128)(2,1)S(1)}, u32[]{:S(2)}, u32[]{:S(2)}) collective-permute-start(bf16[1024,128]{1,0:T(8,128)(2,1)} %get-tuple-element.45), channel_id=1, source_target_pairs={{0,2},{1,3},{2,0},{3,1},{4,6},{5,7},{6,4},{7,5},{8,10},{9,11},{10,... | collective-permute-start | bytes 786440 | tf_op jit(solution)/shard_map/ppermute | solution.py:339
  212.8 13.6 %collective-permute-start.22 = (bf16[512,1024]{1,0:T(8,128)(2,1)}, bf16[512,1024]{1,0:T(8,128)(2,1)S(1)}, u32[]{:S(2)}, u32[]{:S(2)}) collective-permute-start(bf16[512,1024]{1,0:T(8,128)(2,1)} %get-tuple-element.68), channel_id=1, source_target_pairs={{0,8},{8,0},{16,24},{24,16},{32,40},{40,32},{48,56},{56,48},{64,72... | collective-permute-start | bytes 3145736 | tf_op jit(solution)/shard_map/ppermute | solution.py:345
  212.8 70.5 %all-to-all-start.2 = ((bf16[8,1024,128]{2,1,0:T(8,128)(2,1)}), bf16[8,1024,128]{2,1,0:T(8,128)(2,1)S(1)}, u32[]{:S(2)}, u32[]{:S(2)}) async-start(bf16[8,1024,128]{2,1,0:T(8,128)(2,1)} %get-tuple-element.61), calls=%async_computation.2 | async-start | bytes 4194304 | tf_op jit(solution)/shard_map/all_to_all | solution.py:450
  231.3 23.5 %collective-permute-start.23 = (bf16[256,1024]{1,0:T(8,128)(2,1)}, bf16[256,1024]{1,0:T(8,128)(2,1)S(1)}, u32[]{:S(2)}, u32[]{:S(2)}) collective-permute-start(bf16[256,1024]{1,0:T(8,128)(2,1)} %get-tuple-element.71), channel_id=1, source_target_pairs={{0,1},{1,0},{2,3},{3,2},{4,5},{5,4},{6,7},{7,6},{8,9},{9,8},{10,11... | collective-permute-start | bytes 1572872 | tf_op jit(solution)/shard_map/ppermute | solution.py:339
  233.3 33.6 %collective-permute-start.24 = (bf16[256,1024]{1,0:T(8,128)(2,1)}, bf16[256,1024]{1,0:T(8,128)(2,1)}, u32[]{:S(2)}, u32[]{:S(2)}) collective-permute-start(bf16[256,1024]{1,0:T(8,128)(2,1)} %get-tuple-element.72), channel_id=1, source_target_pairs={{0,2},{1,3},{2,0},{3,1},{4,6},{5,7},{6,4},{7,5},{8,10},{9,11},{10,... | collective-permute-start | bytes 1572872 | tf_op jit(solution)/shard_map/ppermute | solution.py:339
  236.0 30.9 %collective-permute-start.25 = (bf16[256,1024]{1,0:T(8,128)(2,1)}, bf16[256,1024]{1,0:T(8,128)(2,1)}, u32[]{:S(2)}, u32[]{:S(2)}) collective-permute-start(bf16[256,1024]{1,0:T(8,128)(2,1)} %get-tuple-element.73), channel_id=1, source_target_pairs={{0,3},{1,2},{2,1},{3,0},{4,7},{5,6},{6,5},{7,4},{8,11},{9,10},{10,... | collective-permute-start | bytes 1572872 | tf_op jit(solution)/shard_map/ppermute | solution.py:339
  270.1 9.3 %collective-permute-start.26 = (bf16[128,1024]{1,0:T(8,128)(2,1)}, bf16[128,1024]{1,0:T(8,128)(2,1)S(1)}, u32[]{:S(2)}, u32[]{:S(2)}) collective-permute-start(bf16[128,1024]{1,0:T(8,128)(2,1)} %get-tuple-element.75), channel_id=1, source_target_pairs={{0,4},{1,5},{2,6},{3,7},{4,0},{5,1},{6,2},{7,3},{8,12},{9,13},{10,... | collective-permute-start | bytes 786440 | tf_op jit(solution)/shard_map/ppermute | solution.py:339
  283.3 21.1 %all-to-all-start.4 = ((bf16[32,48,128]{2,1,0:T(8,128)(2,1)}), bf16[32,48,128]{2,1,0:T(8,128)(2,1)S(1)}, u32[]{:S(2)}, u32[]{:S(2)}) async-start(bf16[32,48,128]{2,1,0:T(8,128)(2,1)} %shard_map.113), calls=%async_computation.4 | async-start | bytes 786432 | tf_op jit(solution)/shard_map/all_to_all | solution.py:505
  (20 other events, 248.3 us)
where the time goes:
time: 312 us; the launch traced here: 309 us
  waiting for transfers between devices  120 us (38%)
  Pallas kernels  90.3 us (29%)
  starting transfers between devices  81 us (26%)
  local copies, waits for them, and re-layouts  15.9 us (5%)
    ppermute x25, waiting for transfers between devices, swap(): lax.ppermute(x, 'chan', [(i, i ^ r) for i in range(n)])  113 us
    ppermute x25, starting transfers between devices, swap(): lax.ppermute(x, 'chan', [(i, i ^ r) for i in range(n)])  45.8 us
    unnamed x48, local copies, waits for them, and re-layouts  13 us
    all_to_all x1, starting transfers between devices, local(): lax.all_to_all(scaled, 'seq', split_axis=0, concat_axis=0, tiled=True)  10.1 us
    pallas_call x1, Pallas kernels, local(): call(functools.partial(kernel_grad_body, heads=heads, n=n, seqs=seqs), (h...  9.15 us
    pallas_call x1, Pallas kernels, local(): call(functools.partial(cot_body, n=n), (n,), [whole(part, width)] * n + [...  8.93 us
    pallas_call x1, Pallas kernels, local(): call(mix_body, (n,), [pair_in, pair_cube, whole(block, block)], [whole(pa...  8.36 us
    pallas_call x1, Pallas kernels, local(): call(functools.partial(gate_body, n=n), (part // chunk,), [pl.BlockSpec((...  7.97 us
  transfers between devices with their start and end apart: 32, of which 16 were waited for; matrix products, arithmetic and copies ran while one was open for 2% of the time, Pallas kernels for 28%

commit v1 on v0

--- a/solution.py
+++ b/solution.py
@@ -25,6 +25,7 @@
         ),
         out_shape=out_shape,
         cost_estimate=pl.CostEstimate(flops=flops, bytes_accessed=nbytes, transcendentals=0),
+        compiler_params=pltpu.CompilerParams(vmem_limit_bytes=48 * 2**20),
     )
 
 
@@ -69,18 +70,18 @@
             outs[q][...] = both
 
 
-def gate_body(me, x_ref, w_ref, mine_ref, peer_ref, *refs, n):
+def gate_body(me, x_ref, near_ref, far_ref, *refs, n):
     gs, wcat, scr = refs[:n], refs[n], refs[n + 1]
 
     @pl.when(pl.program_id(0) == 0)
     def _():
-        half = w_ref.shape[0] // 2
+        half = scr.shape[0] // 2
         near = pl.ds(pl.multiple_of(me[1] * half, half), half)
         far = pl.ds(pl.multiple_of((1 - me[1]) * half, half), half)
-        scr[:, :128] = w_ref[...]
-        for q in range(1, n):
-            scr[near, q * 128 : (q + 1) * 128] = mine_ref[q - 1]
-            scr[far, q * 128 : (q + 1) * 128] = peer_ref[q - 1]
+        ways = near_ref.shape[0]
+        for q in range(n):
+            scr[near, q * 128 : (q + 1) * 128] = near_ref[q % ways, q // ways]
+            scr[far, q * 128 : (q + 1) * 128] = far_ref[q % ways, q // ways]
         wcat[...] = scr[...]
 
     rows_in = lanes([x_ref[r] for r in range(n)])
@@ -109,16 +110,17 @@
 
 
 def back_gate_body(me, *refs, n):
-    os, gs, wcat, tie, h_ref, gp_ref = refs[:n], refs[n : 2 * n], *refs[2 * n :]
+    os, gs, wcat = refs[:n], refs[n : 2 * n], refs[2 * n]
+    hs, gp_ref, hsc = refs[2 * n + 2 : 3 * n + 2], refs[3 * n + 2], refs[3 * n + 3]
     parts = []
     for q in range(n):
         g = gs[q][...].astype(F32)
         parts.append((os[q][...].astype(F32) * g * (1.0 - g)).astype(BF16))
     gp = lanes(parts)
     gp_ref[...] = gp
-    h = lax.dot_general(gp, wcat[...], NT, preferred_element_type=F32).astype(BF16)
-    for d in range(n):
-        h_ref[d] = h[:, d * 128 : (d + 1) * 128]
+    hsc[...] = lax.dot_general(gp, wcat[...], NT, preferred_element_type=F32).astype(BF16)
+    for r in range(n):
+        hs[r][...] = hsc[:, pl.ds(pl.multiple_of((me[0] ^ r) * 128, 128), 128)]
 
 
 def weight_body(me, xt_ref, gp_ref, mine, peer, *, n):
@@ -139,25 +141,13 @@
         put(peer)
 
 
-def add_body(me, a_ref, b_ref, right_ref, left_ref, *outs):
-    ways = len(outs)
-    n, seqs = right_ref.shape[0], right_ref.shape[1]
-    per = a_ref.shape[0] // n
-    size = per + 2 * seqs
-    for r in range(n):
-        out, base = outs[r % ways], (r // ways) * size
+def add_body(me, a_ref, b_ref, left_ref, *outs):
+    per = a_ref.shape[0] // len(outs)
+    for r in range(len(outs)):
         rows = slice(r * per, (r + 1) * per)
         both = a_ref[rows, :].astype(F32) + b_ref[rows, :].astype(F32)
-        out[base : base + per, :] = both.astype(BF16)
-        out[base + per : base + per + seqs, :] = right_ref[r]
-        out[base + per + seqs : base + size, :] = left_ref[r]
-
-
-def mid_body(me, *refs):
-    parts, keep, send = refs[:-2], refs[-2], refs[-1]
-    size = keep.shape[0]
-    keep[...] = total([p[:size, :] for p in parts])
-    send[...] = total([p[size:, :] for p in parts]).astype(BF16)
+        outs[r][:per, :] = both.astype(BF16)
+        outs[r][per:, :] = left_ref[r]
 
 
 def row_order(me, block, n, seqs):
@@ -202,7 +192,7 @@
 
 
 def cot_body(me, *refs, n):
-    gs, og_ref, lt_ref, gv_ref, gm_ref, gsc = refs[:n], *refs[n:]
+    gs, og_ref, lt_ref, tie, gv_ref, gm_ref, gsc = refs[:n], *refs[n:]
     block = lt_ref.shape[0]
     gate_pick(pl.program_id(0), gs, gsc)
     gm = grad_mixed_of(og_ref, gsc, block)
@@ -238,7 +228,8 @@
         put_rows(me, acc, n, seqs, put)
 
 
-def kernel_grad_body(me, d_ref, u_ref, k_ref, x_ref, kg_ref, gu_ref, out, scr, acc, *, heads, n, seqs):
+def kernel_grad_body(me, d_ref, u_ref, k_ref, x_ref, kg_ref, gu_ref, *refs, heads, n, seqs):
+    outs, scr, acc = refs[:n], refs[n], refs[n + 1]
     t = pl.program_id(0)
     step, block = u_ref.shape[0], u_ref.shape[1]
 
@@ -269,28 +260,32 @@
     @pl.when(t == pl.num_programs(0) - 1)
     def _():
         def put(r, low, value):
-            out[r, :, low : low + 128] = value
+            outs[r][:, low : low + 128] = value
 
         put_rows(me, acc, n, seqs, put)
 
 
-def input_grad_body(me, h_ref, gu_ref, rt_ref, out):
+def input_grad_body(me, *refs, n):
+    hs, gu_ref, rt_ref, out, hsc = refs[:n], refs[n], refs[n + 1], refs[n + 2], refs[n + 3]
     block = rt_ref.shape[0]
+    gate_pick(pl.program_id(0), hs, hsc)
     rhs = lanes([gu_ref[u] for u in range(2)])
     back = jnp.dot(rt_ref[...], rhs, preferred_element_type=F32)
     for u in range(2):
         rows = slice(u * block, (u + 1) * block)
-        out[rows, :] = (back[:, u * 128 : (u + 1) * 128] + h_ref[rows, :].astype(F32)).astype(BF16)
+        out[rows, :] = (back[:, u * 128 : (u + 1) * 128] + hsc[rows, :].astype(F32)).astype(BF16)
 
 
 def total(parts):
     return functools.reduce(lambda a, b: a + b, [p.astype(F32) for p in parts])
 
 
-def pack_body(me, keep, got, out, scr, *, seqs, per):
+def pack_body(me, *refs, n, seqs, per):
+    out, scr = refs[2 * n], refs[2 * n + 1]
     slots = out.shape[1]
-    sums = keep[...] + got[...].astype(F32)
-    weight, right, left = sums[:per], sums[per : per + seqs], sums[per + seqs :]
+    sums = total([p[...] for p in refs[:n]])
+    right = total([p[...] for p in refs[n : 2 * n]])
+    weight, left = sums[:per], sums[per:]
     blocks = sums.shape[1] // 128
     for slot in range(blocks):
         cols = slice(slot * 128, (slot + 1) * 128)
@@ -356,7 +351,9 @@
         inputs.reshape(n, part, width), "chan", split_axis=0, concat_axis=0, tiled=True
     )
     half = lax.dynamic_slice_in_dim(gate_weight, core * (model_width // 2), model_width // 2, 0)
-    near = jnp.stack([swap(r, half) for r in range(1, n)])
+    ways = n // 2
+    halves = jnp.stack([half, swap(ways, half)])
+    near = jnp.stack([swap(r, halves) for r in range(ways)])
     far = across(near)
 
     x_cube = inputs.reshape(heads, block, width)
@@ -379,30 +376,19 @@
         functools.partial(gate_body, n=n), (part // chunk,),
         [
             pl.BlockSpec((n, chunk, width), lambda t, me: (0, t, 0)),
-            whole(model_width, width),
-            whole(n - 1, model_width // 2, width),
-            whole(n - 1, model_width // 2, width),
+            whole(n // 2, 2, model_width // 2, width),
+            whole(n // 2, 2, model_width // 2, width),
         ],
         [tok] * n + [whole(model_width, model_width)],
         [S((part, width), BF16)] * n + [S((model_width, model_width), BF16)],
         [pltpu.VMEM((model_width, model_width), BF16)],
         gg, 4 * cube,
-    )(pre, xs, gate_weight, near, far)
+    )(pre, xs, near, far)
     gates_tok, wcat = gate_out[:n], gate_out[n]
     gates = swaps(gates_tok)
 
     pair_in = pl.BlockSpec((seqs, 2, heads, width), lambda t, me: (0, me[0] ^ t, 0, 0))
     pair_cube = pl.BlockSpec((2, block, width), lambda t, me: (me[0] ^ t, 0, 0))
-    grad_mid, grad_mixed = call(
-        functools.partial(cot_body, n=n), (n,),
-        [whole(part, width)] * n + [pair_cube, whole(block, block)],
-        [pair_in, pl.BlockSpec((None, block, 2 * width), lambda t, me: (me[0] ^ t, 0, 0))],
-        [S((seqs, heads, heads, width), BF16), S((n, block, 2 * width), BF16)],
-        [pltpu.VMEM((part, width), BF16)],
-        mm, 4 * cube,
-    )(pre, *gates, og_cube, left_factor.T)
-    grad_back = lax.all_to_all(grad_mid, "seq", split_axis=0, concat_axis=0, tiled=True)
-
     om = call(
         mix_body, (n,),
         [pair_in, pair_cube, whole(block, block)],
@@ -412,6 +398,16 @@
         mm, 3 * cube,
     )(pre, piece, og_cube, left_factor)
     oms = swaps(om)
+
+    grad_mid, grad_mixed = call(
+        functools.partial(cot_body, n=n), (n,),
+        [whole(part, width)] * n + [pair_cube, whole(block, block), tie],
+        [pair_in, pl.BlockSpec((None, block, 2 * width), lambda t, me: (me[0] ^ t, 0, 0))],
+        [S((seqs, heads, heads, width), BF16), S((n, block, 2 * width), BF16)],
+        [pltpu.VMEM((part, width), BF16)],
+        mm, 4 * cube,
+    )(pre, *gates, og_cube, left_factor.T, om[0])
+    grad_back = lax.all_to_all(grad_mid, "seq", split_axis=0, concat_axis=0, tiled=True)
 
     count = block * block // (n * seqs * 128)
     lefts = call(
@@ -436,18 +432,15 @@
         gg, 2 * cube,
     )(pre, xs)
 
-    back_gate, grad_pre = call(
+    back_out = call(
         functools.partial(back_gate_body, n=n), (part // chunk,),
         [tok] * n + [tok] * n + [whole(model_width, model_width), tie],
-        [
-            pl.BlockSpec((n, chunk, width), lambda t, me: (0, t, 0)),
-            pl.BlockSpec((chunk, model_width), lambda t, me: (t, 0)),
-        ],
-        [S((n, part, width), BF16), S((part, model_width), BF16)],
-        [],
+        [tok] * n + [pl.BlockSpec((chunk, model_width), lambda t, me: (t, 0))],
+        [S((part, width), BF16)] * n + [S((part, model_width), BF16)],
+        [pltpu.VMEM((chunk, model_width), BF16)],
         gg, 5 * cube,
     )(pre, *oms, *gates_tok, wcat, lefts)
-    gate_in = lax.all_to_all(back_gate, "chan", split_axis=0, concat_axis=0, tiled=True)
+    grad_pre = back_out[n]
 
     quarter = (model_width // 4, model_width)
     mine, other = call(
@@ -464,58 +457,50 @@
         [],
         gg, 3 * cube,
     )(pre, turned, grad_pre)
-    kernel_grad, grad_first, rights = call(
+    per = model_width // (2 * n)
+    size = per + seqs
+    sums_out = call(
+        add_body, (1,),
+        [whole(model_width // 2, model_width)] * 2 + [whole(n, seqs, count * 128)],
+        [whole(size, model_width)] * n,
+        [S((size, model_width), BF16)] * n,
+        [],
+        cube, 2 * cube,
+    )(pre, mine, across(other), lefts)
+    sums = swaps(sums_out)
+    hs = swaps(back_out[:n])
+
+    kernel_out = call(
         functools.partial(kernel_grad_body, heads=heads, n=n, seqs=seqs), (heads // step,),
         [whole(seqs, heads, heads, width), four, four, four],
-        [four, four, whole(n, seqs, count * 128)],
-        [S((heads, block, width), BF16)] * 2 + [S((n, seqs, count * 128), BF16)],
+        [four, four] + [whole(seqs, count * 128)] * n,
+        [S((heads, block, width), BF16)] * 2 + [S((seqs, count * 128), BF16)] * n,
         [pltpu.VMEM((block * heads, width), F32), pltpu.VMEM((block, block), F32)],
         mm, 6 * cube,
     )(pre, grad_back, first, kernel, x_cube)
 
-    ways = n // 2
-    per = model_width // (2 * n)
-    size = per + 2 * seqs
-    pieces = call(
-        add_body, (1,),
-        [whole(model_width // 2, model_width)] * 2 + [whole(n, seqs, count * 128)] * 2,
-        [whole(2 * size, model_width)] * ways,
-        [S((2 * size, model_width), BF16)] * ways,
-        [],
-        cube, 3 * cube,
-    )(pre, mine, across(other), rights, lefts)
-    keep, send = call(
-        mid_body, (1,),
-        [whole(2 * size, model_width)] * ways,
-        [whole(size, model_width)] * 2,
-        [S((size, model_width), F32), S((size, model_width), BF16)],
-        [],
-        cube, 2 * cube,
-    )(pre, *[swap(r, pieces[r]) for r in range(ways)])
+    kernel_grad, grad_first = kernel_out[:2]
+    rights = swaps(kernel_out[2:])
 
     slots = 2 * count + model_width * model_width // (n * seqs * 128)
     packed = call(
-        functools.partial(pack_body, seqs=seqs, per=per), (1,),
-        [whole(size, model_width)] * 2,
+        functools.partial(pack_body, n=n, seqs=seqs, per=per), (1,),
+        [whole(size, model_width)] * n + [whole(seqs, model_width)] * n,
         whole(seqs, slots, 128),
         S((seqs, slots, 128), BF16),
         [pltpu.VMEM((seqs * slots, 128), F32)],
         cube, cube,
-    )(pre, keep, swap(ways, send))
+    )(pre, *sums, *rights)
     got = lax.all_to_all(packed, "seq", split_axis=0, concat_axis=0, tiled=True)
 
     input_grad = call(
-        input_grad_body, (n,),
-        [
-            pl.BlockSpec((None, part, width), lambda t, me: (t, 0, 0)),
-            pl.BlockSpec((2, block, width), lambda t, me: (t, 0, 0)),
-            whole(block, block),
-        ],
-        pl.BlockSpec((part, width), lambda t, me: (t, 0)),
+        functools.partial(input_grad_body, n=n), (n,),
+        [whole(part, width)] * n + [pair_cube, whole(block, block)],
+        pl.BlockSpec((part, width), lambda t, me: (me[0] ^ t, 0)),
         S((rows, width), BF16),
-        [],
+        [pltpu.VMEM((part, width), BF16)],
         mm, 3 * cube,
-    )(pre, gate_in, grad_first, right_factor.T)
+    )(pre, *hs, grad_first, right_factor.T)
 
     left_share, right_share, weight_share = call(
         functools.partial(

time: 312 us -> 331 us (1.061)
  starting transfers between devices: 81 us -> 108 us
  Pallas kernels: 90.3 us -> 68.9 us
  local copies, waits for them, and re-layouts: 15.9 us -> 23 us
  waiting for transfers between devices: 120 us -> 127 us
    ppermute x25 -> x39, starting transfers between devices: 45.8 us -> 75.8 us  [swap(): lax.ppermute(x, 'chan', [(i, i ^ r) for i in range(n)])]
    all_to_all x1, waiting for transfers between devices: 0.01 us -> 22.2 us  [local(): lax.all_to_all(scaled, 'seq', split_axis=0, concat_axis=0, tiled=True)]
    ppermute x25 -> x39, waiting for transfers between devices: 113 us -> 99.6 us  [swap(): lax.ppermute(x, 'chan', [(i, i ^ r) for i in range(n)])]
    unnamed x48 -> x96, local copies, waits for them, and re-layouts: 13 us -> 22.4 us
    all_to_all x1, waiting for transfers between devices: 5.6 us -> 0.01 us  [local(): got = lax.all_to_all(packed, 'seq', split_axis=0, concat_axis=0, tiled=True)]
    pallas_call x3 -> x2, Pallas kernels: 14.3 us -> 9.75 us  [the longest x1 6.35 us: local(): call(functools.partial(input_grad_body, n=n), (n,), [whole(part, width)]...]
    all_to_all x1 -> x0, starting transfers between devices: 4.48 us -> none  [local(): lax.all_to_all(back_gate, 'chan', split_axis=0, concat_axis=0, tiled=True)]
    ppermute x2, waiting for transfers between devices: 2.1 us -> 5.57 us  [across(): return lax.ppermute(x, 'seq', [(i, i ^ 1) for i in range(seqs)])]
  transfers between devices with their start and end apart: 32 -> 45, of which waited for: 16 -> 19; matrix products, arithmetic and copies ran while one was open for 2% -> 1% of each run, Pallas kernels for 28% -> 17%
where the time goes in v1:
time: 331 us; the launch traced here: 329 us
  waiting for transfers between devices  127 us (38%)
  starting transfers between devices  108 us (33%)
  Pallas kernels  68.9 us (21%)
  local copies, waits for them, and re-layouts  23 us (7%)
    ppermute x39, waiting for transfers between devices, swap(): lax.ppermute(x, 'chan', [(i, i ^ r) for i in range(n)])  99.6 us
    ppermute x39, starting transfers between devices, swap(): lax.ppermute(x, 'chan', [(i, i ^ r) for i in range(n)])  75.8 us
    unnamed x96, local copies, waits for them, and re-layouts  22.4 us
    all_to_all x1, waiting for transfers between devices, local(): lax.all_to_all(scaled, 'seq', split_axis=0, concat_axis=0, tiled=True)  22.2 us
    all_to_all x1, starting transfers between devices, local(): lax.all_to_all(scaled, 'seq', split_axis=0, concat_axis=0, tiled=True)  10.1 us
    all_to_all x1, starting transfers between devices, local(): got = lax.all_to_all(packed, 'seq', split_axis=0, concat_axis=0, tiled=True)  9.45 us
    pallas_call x1, Pallas kernels, local(): call(functools.partial(kernel_grad_body, heads=heads, n=n, seqs=seqs), (h...  8.19 us
    pallas_call x1, Pallas kernels, local(): call(functools.partial(cot_body, n=n), (n,), [whole(part, width)] * n + [...  7.95 us
  transfers between devices with their start and end apart: 45, of which 19 were waited for; matrix products, arithmetic and copies ran while one was open for 1% of the time, Pallas kernels for 17%

profile of v1, /device:TPU:2, one launch (start us, length us, event | category | flops | bytes accessed | tf_op | source)
XLA Modules:
  0.0 329.4 jit_solution(12633795913188069580)
XLA Ops:
  0.6 6.2 %all-to-all-start.1 = ((bf16[8,1024,128]{2,1,0:T(8,128)(2,1)}), bf16[8,1024,128]{2,1,0:T(8,128)(2,1)S(1)}, u32[]{:S(2)}, u32[]{:S(2)}) async-start(bf16[8,1024,128]{2,1,0:T(8,128)(2,1)} %bitcast.19), calls=%async_computation.1 | async-start | bytes 4194304 | tf_op jit(solution)/shard_map/all_to_all | solution.py:350
  6.9 3.6 %collective-permute-start = (bf16[512,128]{1,0:T(8,128)(2,1)S(1)}, bf16[512,128]{1,0:T(8,128)(2,1)S(1)}, u32[]{:S(2)}, u32[]{:S(2)}) collective-permute-start(bf16[512,128]{1,0:T(8,128)(2,1)S(1)} %constant_dynamic-slice_fusion), channel_id=1, source_target_pairs={{0,4},{1,5},{2,6},{3,7},{4,0},{5,1},{6,2},{7,3},{8,12},{9,13},{10,... | collective-permute-start | bytes 393224 | tf_op jit(solution)/shard_map/ppermute | solution.py:334
  10.5 25.6 %collective-permute-done = bf16[512,128]{1,0:T(8,128)(2,1)S(1)} collective-permute-done((bf16[512,128]{1,0:T(8,128)(2,1)S(1)}, bf16[512,128]{1,0:T(8,128)(2,1)S(1)}, u32[]{:S(2)}, u32[]{:S(2)}) %collective-permute-start) | collective-permute-done | bytes 131104 | tf_op jit(solution)/shard_map/ppermute | solution.py:334
  40.3 9.6 %collective-permute-done.3 = bf16[2,512,128]{2,1,0:T(8,128)(2,1)S(1)} collective-permute-done((bf16[2,512,128]{2,1,0:T(8,128)(2,1)S(1)}, bf16[2,512,128]{2,1,0:T(8,128)(2,1)S(1)}, u32[]{:S(2)}, u32[]{:S(2)}) %collective-permute-start.3) | collective-permute-done | bytes 262176 | tf_op jit(solution)/shard_map/ppermute | solution.py:334
  54.7 5.4 %shard_map.101 = (bf16[16,512,128]{2,1,0:T(8,128)(2,1)S(1)}, bf16[32,16,16,128]{3,2,1,0:T(8,128)(2,1)S(1)}) custom-call(s32[2]{0:T(128)S(1)} %pad_add_fusion.me, bf16[16,512,128]{2,1,0:T(8,128)(2,1)} %bitcast.20, bf16[16,512,128]{2,1,0:T(8,128)(2,1)} %k_ref.3, bf16[512,512]{1,0:T(8,128)(2,1)S(1)} %copy-done.2, ...), custom_call_target="tpu_custom_call" | custom-call | flops 1073741824 | bytes 8388608 | tf_op jit(solution)/shard_map/pallas_call | solution.py:363
  64.1 10.1 %all-to-all-start = ((bf16[32,16,16,128]{3,2,1,0:T(8,128)(2,1)}), bf16[32,16,16,128]{3,2,1,0:T(8,128)(2,1)S(1)}, u32[]{:S(2)}, u32[]{:S(2)}) async-start(bf16[32,16,16,128]{3,2,1,0:T(8,128)(2,1)} %copy-done.7), calls=%async_computation | async-start | bytes 4194304 | tf_op jit(solution)/shard_map/all_to_all | solution.py:371
  74.2 7.6 %shard_map.103 = (bf16[1024,128]{1,0:T(8,128)(2,1)S(1)}, bf16[1024,128]{1,0:T(8,128)(2,1)S(1)}, bf16[1024,128]{1,0:T(8,128)(2,1)S(1)}, bf16[1024,128]{1,0:T(8,12...) custom-call(s32[2]{0:T(128)S(1)} %pad_add_fusion.me, ...), custom_call_target="tpu_custom_call" | custom-call | flops 2147483648 | bytes 8388608 | tf_op jit(solution)/shard_map/pallas_call | solution.py:375
  92.4 4.2 %collective-permute-start.17 = (bf16[1024,128]{1,0:T(8,128)(2,1)}, bf16[1024,128]{1,0:T(8,128)(2,1)}, u32[]{:S(2)}, u32[]{:S(2)}) collective-permute-start(bf16[1024,128]{1,0:T(8,128)(2,1)} %get-tuple-element.73.refs_14_), channel_id=1, source_target_pairs={{0,6},{1,7},{2,4},{3,5},{4,2},{5,3},{6,0},{7,1},{8,14},{9,15},{10,... | collective-permute-start | bytes 786440 | tf_op jit(solution)/shard_map/ppermute | solution.py:334
  101.0 22.2 %all-to-all-done.p_ref = bf16[32,16,16,128]{3,2,1,0:T(8,128)(2,1)S(1)} async-done(((bf16[32,16,16,128]{3,2,1,0:T(8,128)(2,1)}), bf16[32,16,16,128]{3,2,1,0:T(8,128)(2,1)S(1)}, u32[]{:S(2)}, u32[]{:S(2)}) %all-to-all-start) | async-done | bytes 2097184 | tf_op jit(solution)/shard_map/all_to_all | solution.py:371
  123.2 6.4 %shard_map.102 = (bf16[1024,128]{1,0:T(8,128)(2,1)S(1)}, bf16[1024,128]{1,0:T(8,128)(2,1)S(1)}, bf16[1024,128]{1,0:T(8,128)(2,1)S(1)}, bf16[1024,128]{1,0:T(8,12...) custom-call(s32[2]{0:T(128)S(1)} %pad_add_fusion.me, ...), custom_call_target="tpu_custom_call" | custom-call | flops 1073741824 | bytes 6291456 | tf_op jit(solution)/shard_map/pallas_call | solution.py:392
  134.7 7.9 %shard_map.104 = (bf16[32,16,16,128]{3,2,1,0:T(8,128)(2,1)S(1)}, bf16[8,512,256]{2,1,0:T(8,128)(2,1)}) custom-call(s32[2]{0:T(128)S(1)} %pad_add_fusion.me, bf16[1024,128]{1,0:T(8,128)(2,1)S(1)} %copy-done.17, bf16[1024,128]{1,0:T(8,128)(2,1)S(1)} %copy-done.20, bf16[1024,128]{1,0:T(8,128)(2,1)S(1)} %copy-done.22, ...), custom_call_target="tpu_custom_call" | custom-call | flops 1073741824 | bytes 8388608 | tf_op jit(solution)/shard_map/pallas_call | solution.py:402
  144.0 6.1 %all-to-all-start.2 = ((bf16[32,16,16,128]{3,2,1,0:T(8,128)(2,1)}), bf16[32,16,16,128]{3,2,1,0:T(8,128)(2,1)}, u32[]{:S(2)}, u32[]{:S(2)}) async-start(bf16[32,16,16,128]{3,2,1,0:T(8,128)(2,1)} %copy-done.6), calls=%async_computation.2 | async-start | bytes 4194304 | tf_op jit(solution)/shard_map/all_to_all | solution.py:410
  162.5 4.3 %collective-permute-done.6.refs_2_ = bf16[1024,128]{1,0:T(8,128)(2,1)S(1)} collective-permute-done((bf16[1024,128]{1,0:T(8,128)(2,1)}, bf16[1024,128]{1,0:T(8,128)(2,1)S(1)}, u32[]{:S(2)}, u32[]{:S(2)}) %collective-permute-start.6) | collective-permute-done | bytes 262176 | tf_op jit(solution)/shard_map/ppermute | solution.py:334
  168.7 4.3 %shard_map.109.xt_ref = bf16[1024,1024]{1,0:T(8,128)(2,1)S(1)} custom-call(s32[2]{0:T(128)S(1)} %pad_add_fusion.me, bf16[8,1024,128]{2,1,0:T(8,128)(2,1)S(1)} %copy-done.5), custom_call_target="tpu_custom_call" | custom-call | flops 2147483648 | bytes 4194304 | tf_op jit(solution)/shard_map/pallas_call | solution.py:426
  173.1 3.4 %shard_map.105.refs_17_.left_ref = bf16[8,32,1024]{2,1,0:T(8,128)(2,1)S(1)} custom-call(s32[2]{0:T(128)S(1)} %pad_add_fusion.me, bf16[8,512,256]{2,1,0:T(8,128)(2,1)S(1)} %copy-done.8, bf16[32,16,16,128]{3,2,1,0:T(8,128)(2,1)S(1)} %all-to-all-done.p_ref, bf16[1024,128]{1,0:T(8,128)(2,1)S(1)} %copy-done.13), custom_call_target="tpu_custom_call" | custom-call | flops 1073741824 | bytes 4194304 | tf_op jit(solution)/shard_map/pallas_call | solution.py:413
  179.2 12.9 %collective-permute-done.10.refs_6_ = bf16[1024,128]{1,0:T(8,128)(2,1)S(1)} collective-permute-done((bf16[1024,128]{1,0:T(8,128)(2,1)S(1)}, bf16[1024,128]{1,0:T(8,128)(2,1)S(1)}, u32[]{:S(2)}, u32[]{:S(2)}) %collective-permute-start.10) | collective-permute-done | bytes 262176 | tf_op jit(solution)/shard_map/ppermute | solution.py:334
  192.2 7.5 %collective-permute-done.11.refs_7_ = bf16[1024,128]{1,0:T(8,128)(2,1)S(1)} collective-permute-done((bf16[1024,128]{1,0:T(8,128)(2,1)S(1)}, bf16[1024,128]{1,0:T(8,128)(2,1)S(1)}, u32[]{:S(2)}, u32[]{:S(2)}) %collective-permute-start.11) | collective-permute-done | bytes 262176 | tf_op jit(solution)/shard_map/ppermute | solution.py:334
  199.7 6.3 %shard_map.106 = (bf16[1024,128]{1,0:T(8,128)(2,1)S(1)}, bf16[1024,128]{1,0:T(8,128)(2,1)S(1)}, bf16[1024,128]{1,0:T(8,128)(2,1)S(1)}, bf16[1024,128]{1,0:T(8,12...) custom-call(s32[2]{0:T(128)S(1)} %pad_add_fusion.me, ...), custom_call_target="tpu_custom_call" | custom-call | flops 2147483648 | bytes 10485760 | tf_op jit(solution)/shard_map/pallas_call | solution.py:435
  206.8 5.7 %shard_map.110 = (bf16[512,1024]{1,0:T(8,128)(2,1)S(1)}, bf16[512,1024]{1,0:T(8,128)(2,1)S(1)}) custom-call(s32[2]{0:T(128)S(1)} %pad_add_fusion.me, bf16[1024,1024]{1,0:T(8,128)(2,1)S(1)} %shard_map.109.xt_ref, bf16[1024,1024]{1,0:T(8,128)(2,1)} %get-tuple-element.89.gp_ref), custom_call_target="tpu_custom_call" | custom-call | flops 2147483648 | bytes 6291456 | tf_op jit(solution)/shard_map/pallas_call | solution.py:446
  228.7 9.7 %collective-permute-start.33 = (bf16[96,1024]{1,0:T(8,128)(2,1)}, bf16[96,1024]{1,0:T(8,128)(2,1)}, u32[]{:S(2)}, u32[]{:S(2)}) collective-permute-start(bf16[96,1024]{1,0:T(8,128)(2,1)} %get-tuple-element.99), channel_id=1, source_target_pairs={{0,7},{1,6},{2,5},{3,4},{4,3},{5,2},{6,1},{7,0},{8,15},{9,14},{10,... | collective-permute-start | bytes 589832 | tf_op jit(solution)/shard_map/ppermute | solution.py:334
  238.4 8.2 %shard_map.107 = (bf16[16,512,128]{2,1,0:T(8,128)(2,1)}, bf16[16,512,128]{2,1,0:T(8,128)(2,1)S(1)}, bf16[32,1024]{1,0:T(8,128)(2,1)S(1)}, bf16[32,1024]{1,0:T(8,...) custom-call(s32[2]{0:T(128)S(1)} %pad_add_fusion.me, ...), custom_call_target="tpu_custom_call" | custom-call | flops 1073741824 | bytes 12582912 | tf_op jit(solution)/shard_map/pallas_call | solution.py:473
  247.6 3.7 %collective-permute-start.36 = (bf16[32,1024]{1,0:T(8,128)(2,1)S(1)}, bf16[32,1024]{1,0:T(8,128)(2,1)S(1)}, u32[]{:S(2)}, u32[]{:S(2)}) collective-permute-start(bf16[32,1024]{1,0:T(8,128)(2,1)S(1)} %get-tuple-element.103), channel_id=1, source_target_pairs={{0,3},{1,2},{2,1},{3,0},{4,7},{5,6},{6,5},{7,4},{8,11},{9,10},{10,... | collective-permute-start | bytes 196616 | tf_op jit(solution)/shard_map/ppermute | solution.py:334
  253.9 4.0 %collective-permute-start.39 = (bf16[32,1024]{1,0:T(8,128)(2,1)S(1)}, bf16[32,1024]{1,0:T(8,128)(2,1)S(1)}, u32[]{:S(2)}, u32[]{:S(2)}) collective-permute-start(bf16[32,1024]{1,0:T(8,128)(2,1)S(1)} %get-tuple-element.106), channel_id=1, source_target_pairs={{0,6},{1,7},{2,4},{3,5},{4,2},{5,3},{6,0},{7,1},{8,14},{9,15},{10,... | collective-permute-start | bytes 196616 | tf_op jit(solution)/shard_map/ppermute | solution.py:334
  257.8 3.6 %collective-permute-start.40 = (bf16[32,1024]{1,0:T(8,128)(2,1)S(1)}, bf16[32,1024]{1,0:T(8,128)(2,1)S(1)}, u32[]{:S(2)}, u32[]{:S(2)}) collective-permute-start(bf16[32,1024]{1,0:T(8,128)(2,1)S(1)} %get-tuple-element.107), channel_id=1, source_target_pairs={{0,7},{1,6},{2,5},{3,4},{4,3},{5,2},{6,1},{7,0},{8,15},{9,14},{10,... | collective-permute-start | bytes 196616 | tf_op jit(solution)/shard_map/ppermute | solution.py:334
  262.1 3.6 %collective-permute-done.40.refs_15_ = bf16[32,1024]{1,0:T(8,128)(2,1)S(1)} collective-permute-done((bf16[32,1024]{1,0:T(8,128)(2,1)S(1)}, bf16[32,1024]{1,0:T(8,128)(2,1)S(1)}, u32[]{:S(2)}, u32[]{:S(2)}) %collective-permute-start.40) | collective-permute-done | bytes 65568 | tf_op jit(solution)/shard_map/ppermute | solution.py:334
  265.7 3.4 %shard_map.112 = bf16[32,48,128]{2,1,0:T(8,128)(2,1)} custom-call(s32[2]{0:T(128)S(1)} %pad_add_fusion.me, bf16[96,1024]{1,0:T(8,128)(2,1)S(1)} %get-tuple-element.92.refs_0_, bf16[96,1024]{1,0:T(8,128)(2,1)S(1)} %collective-permute-done.27.refs_1_, bf16[96,1024]{1,0:T(8,128)(2,1)S(1)} %collective-permute-done.28.refs_2_, ...), custom_call_target="tpu_custom_call" | custom-call | flops 2097152 | bytes 2097152 | tf_op jit(solution)/shard_map/pallas_call | solution.py:486
  269.1 9.5 %all-to-all-start.3 = ((bf16[32,48,128]{2,1,0:T(8,128)(2,1)}), bf16[32,48,128]{2,1,0:T(8,128)(2,1)}, u32[]{:S(2)}, u32[]{:S(2)}) async-start(bf16[32,48,128]{2,1,0:T(8,128)(2,1)} %shard_map.112), calls=%async_computation.3 | async-start | bytes 786432 | tf_op jit(solution)/shard_map/all_to_all | solution.py:494
  278.7 4.6 %collective-permute-start.20 = (bf16[1024,128]{1,0:T(8,128)(2,1)}, bf16[1024,128]{1,0:T(8,128)(2,1)S(1)}, u32[]{:S(2)}, u32[]{:S(2)}) collective-permute-start(bf16[1024,128]{1,0:T(8,128)(2,1)} %copy-done.32), channel_id=1, source_target_pairs={{0,2},{1,3},{2,0},{3,1},{4,6},{5,7},{6,4},{7,5},{8,10},{9,11},{10,... | collective-permute-start | bytes 786440 | tf_op jit(solution)/shard_map/ppermute | solution.py:334
  288.7 3.2 collective-permute-start.24
  291.9 14.3 %collective-permute-done.20.refs_2_ = bf16[1024,128]{1,0:T(8,128)(2,1)S(1)} collective-permute-done((bf16[1024,128]{1,0:T(8,128)(2,1)}, bf16[1024,128]{1,0:T(8,128)(2,1)S(1)}, u32[]{:S(2)}, u32[]{:S(2)}) %collective-permute-start.20) | collective-permute-done | bytes 262176 | tf_op jit(solution)/shard_map/ppermute | solution.py:334
  307.2 10.0 %collective-permute-done.25.refs_7_ = bf16[1024,128]{1,0:T(8,128)(2,1)} collective-permute-done((bf16[1024,128]{1,0:T(8,128)(2,1)}, bf16[1024,128]{1,0:T(8,128)(2,1)}, u32[]{:S(2)}, u32[]{:S(2)}) %collective-permute-start.25) | collective-permute-done | bytes 262176 | tf_op jit(solution)/shard_map/ppermute | solution.py:334
  320.1 6.4 %shard_map.108 = bf16[8192,128]{1,0:T(8,128)(2,1)} custom-call(s32[2]{0:T(128)S(1)} %pad_add_fusion.me, bf16[1024,128]{1,0:T(8,128)(2,1)S(1)} %copy-done.15, bf16[1024,128]{1,0:T(8,128)(2,1)S(1)} %copy-done.24, bf16[1024,128]{1,0:T(8,128)(2,1)S(1)} %copy-done.26, bf16[1024,128]{1,0:T(8,128)(2,1)} %collective-permute-done.21.refs_3_, ...), custom_call_target="tpu_custom_call" | custom-call | flops 1073741824 | bytes 6291456 | tf_op jit(solution)/shard_map/pallas_call | solution.py:496
  (173 shorter events, 84.8 us)
Async XLA Ops:
  0.6 62.1 %all-to-all-start.1 = ((bf16[8,1024,128]{2,1,0:T(8,128)(2,1)}), bf16[8,1024,128]{2,1,0:T(8,128)(2,1)S(1)}, u32[]{:S(2)}, u32[]{:S(2)}) async-start(bf16[8,1024,128]{2,1,0:T(8,128)(2,1)} %bitcast.19), calls=%async_computation.1 | async-start | bytes 4194304 | tf_op jit(solution)/shard_map/all_to_all | solution.py:350
  6.9 29.2 %collective-permute-start = (bf16[512,128]{1,0:T(8,128)(2,1)S(1)}, bf16[512,128]{1,0:T(8,128)(2,1)S(1)}, u32[]{:S(2)}, u32[]{:S(2)}) collective-permute-start(bf16[512,128]{1,0:T(8,128)(2,1)S(1)} %constant_dynamic-slice_fusion), channel_id=1, source_target_pairs={{0,4},{1,5},{2,6},{3,7},{4,0},{5,1},{6,2},{7,3},{8,12},{9,13},{10,... | collective-permute-start | bytes 393224 | tf_op jit(solution)/shard_map/ppermute | solution.py:334
  36.1 13.8 %collective-permute-start.3 = (bf16[2,512,128]{2,1,0:T(8,128)(2,1)S(1)}, bf16[2,512,128]{2,1,0:T(8,128)(2,1)S(1)}, u32[]{:S(2)}, u32[]{:S(2)}) collective-permute-start(bf16[2,512,128]{2,1,0:T(8,128)(2,1)S(1)} %get-tuple-element.112), channel_id=1, source_target_pairs={{0,3},{1,2},{2,1},{3,0},{4,7},{5,6},{6,5},{7,4},{8,11},{9,10},{10,... | collective-permute-start | bytes 786440 | tf_op jit(solution)/shard_map/ppermute | solution.py:334
  39.7 10.9 %collective-permute-start.1 = (bf16[2,512,128]{2,1,0:T(8,128)(2,1)S(1)}, bf16[2,512,128]{2,1,0:T(8,128)(2,1)S(1)}, u32[]{:S(2)}, u32[]{:S(2)}) collective-permute-start(bf16[2,512,128]{2,1,0:T(8,128)(2,1)S(1)} %get-tuple-element.112), channel_id=1, source_target_pairs={{0,1},{1,0},{2,3},{3,2},{4,5},{5,4},{6,7},{7,6},{8,9},{9,8},{10,11... | collective-permute-start | bytes 786440 | tf_op jit(solution)/shard_map/ppermute | solution.py:334
  64.1 59.1 %all-to-all-start = ((bf16[32,16,16,128]{3,2,1,0:T(8,128)(2,1)}), bf16[32,16,16,128]{3,2,1,0:T(8,128)(2,1)S(1)}, u32[]{:S(2)}, u32[]{:S(2)}) async-start(bf16[32,16,16,128]{3,2,1,0:T(8,128)(2,1)} %copy-done.7), calls=%async_computation | async-start | bytes 4194304 | tf_op jit(solution)/shard_map/all_to_all | solution.py:371
  84.5 14.3 %collective-permute-start.13 = (bf16[1024,128]{1,0:T(8,128)(2,1)S(1)}, bf16[1024,128]{1,0:T(8,128)(2,1)S(1)}, u32[]{:S(2)}, u32[]{:S(2)}) collective-permute-start(bf16[1024,128]{1,0:T(8,128)(2,1)S(1)} %get-tuple-element.69.refs_10_), channel_id=1, source_target_pairs={{0,2},{1,3},{2,0},{3,1},{4,6},{5,7},{6,4},{7,5},{8,10},{9,11},{10,... | collective-permute-start | bytes 786440 | tf_op jit(solution)/shard_map/ppermute | solution.py:334
  88.2 46.4 %collective-permute-start.14 = (bf16[1024,128]{1,0:T(8,128)(2,1)}, bf16[1024,128]{1,0:T(8,128)(2,1)}, u32[]{:S(2)}, u32[]{:S(2)}) collective-permute-start(bf16[1024,128]{1,0:T(8,128)(2,1)} %get-tuple-element.70.refs_11_), channel_id=1, source_target_pairs={{0,3},{1,2},{2,1},{3,0},{4,7},{5,6},{6,5},{7,4},{8,11},{9,10},{10,... | collective-permute-start | bytes 786440 | tf_op jit(solution)/shard_map/ppermute | solution.py:334
  88.6 46.0 %collective-permute-start.15 = (bf16[1024,128]{1,0:T(8,128)(2,1)}, bf16[1024,128]{1,0:T(8,128)(2,1)}, u32[]{:S(2)}, u32[]{:S(2)}) collective-permute-start(bf16[1024,128]{1,0:T(8,128)(2,1)} %get-tuple-element.71.refs_12_), channel_id=1, source_target_pairs={{0,4},{1,5},{2,6},{3,7},{4,0},{5,1},{6,2},{7,3},{8,12},{9,13},{10,... | collective-permute-start | bytes 786440 | tf_op jit(solution)/shard_map/ppermute | solution.py:334
  89.1 45.5 %collective-permute-start.16 = (bf16[1024,128]{1,0:T(8,128)(2,1)}, bf16[1024,128]{1,0:T(8,128)(2,1)}, u32[]{:S(2)}, u32[]{:S(2)}) collective-permute-start(bf16[1024,128]{1,0:T(8,128)(2,1)} %get-tuple-element.72.refs_13_), channel_id=1, source_target_pairs={{0,5},{1,4},{2,7},{3,6},{4,1},{5,0},{6,3},{7,2},{8,13},{9,12},{10,... | collective-permute-start | bytes 786440 | tf_op jit(solution)/shard_map/ppermute | solution.py:334
  92.4 42.2 %collective-permute-start.17 = (bf16[1024,128]{1,0:T(8,128)(2,1)}, bf16[1024,128]{1,0:T(8,128)(2,1)}, u32[]{:S(2)}, u32[]{:S(2)}) collective-permute-start(bf16[1024,128]{1,0:T(8,128)(2,1)} %get-tuple-element.73.refs_14_), channel_id=1, source_target_pairs={{0,6},{1,7},{2,4},{3,5},{4,2},{5,3},{6,0},{7,1},{8,14},{9,15},{10,... | collective-permute-start | bytes 786440 | tf_op jit(solution)/shard_map/ppermute | solution.py:334
  99.5 35.1 %collective-permute-start.18 = (bf16[1024,128]{1,0:T(8,128)(2,1)}, bf16[1024,128]{1,0:T(8,128)(2,1)}, u32[]{:S(2)}, u32[]{:S(2)}) collective-permute-start(bf16[1024,128]{1,0:T(8,128)(2,1)} %get-tuple-element.74.refs_15_), channel_id=1, source_target_pairs={{0,7},{1,6},{2,5},{3,4},{4,3},{5,2},{6,1},{7,0},{8,15},{9,14},{10,... | collective-permute-start | bytes 786440 | tf_op jit(solution)/shard_map/ppermute | solution.py:334
  144.0 94.4 %all-to-all-start.2 = ((bf16[32,16,16,128]{3,2,1,0:T(8,128)(2,1)}), bf16[32,16,16,128]{3,2,1,0:T(8,128)(2,1)}, u32[]{:S(2)}, u32[]{:S(2)}) async-start(bf16[32,16,16,128]{3,2,1,0:T(8,128)(2,1)} %copy-done.6), calls=%async_computation.2 | async-start | bytes 4194304 | tf_op jit(solution)/shard_map/all_to_all | solution.py:410
  151.6 15.2 %collective-permute-start.6 = (bf16[1024,128]{1,0:T(8,128)(2,1)}, bf16[1024,128]{1,0:T(8,128)(2,1)S(1)}, u32[]{:S(2)}, u32[]{:S(2)}) collective-permute-start(bf16[1024,128]{1,0:T(8,128)(2,1)} %copy-done.45), channel_id=1, source_target_pairs={{0,2},{1,3},{2,0},{3,1},{4,6},{5,7},{6,4},{7,5},{8,10},{9,11},{10,... | collective-permute-start | bytes 786440 | tf_op jit(solution)/shard_map/ppermute | solution.py:334
  154.5 22.8 %collective-permute-start.7 = (bf16[1024,128]{1,0:T(8,128)(2,1)}, bf16[1024,128]{1,0:T(8,128)(2,1)S(1)}, u32[]{:S(2)}, u32[]{:S(2)}) collective-permute-start(bf16[1024,128]{1,0:T(8,128)(2,1)} %copy-done.44), channel_id=1, source_target_pairs={{0,3},{1,2},{2,1},{3,0},{4,7},{5,6},{6,5},{7,4},{8,11},{9,10},{10,... | collective-permute-start | bytes 786440 | tf_op jit(solution)/shard_map/ppermute | solution.py:334
  154.9 22.4 %collective-permute-start.8 = (bf16[1024,128]{1,0:T(8,128)(2,1)}, bf16[1024,128]{1,0:T(8,128)(2,1)S(1)}, u32[]{:S(2)}, u32[]{:S(2)}) collective-permute-start(bf16[1024,128]{1,0:T(8,128)(2,1)} %copy-done.43), channel_id=1, source_target_pairs={{0,4},{1,5},{2,6},{3,7},{4,0},{5,1},{6,2},{7,3},{8,12},{9,13},{10,... | collective-permute-start | bytes 786440 | tf_op jit(solution)/shard_map/ppermute | solution.py:334
  155.5 23.7 %collective-permute-start.9 = (bf16[1024,128]{1,0:T(8,128)(2,1)}, bf16[1024,128]{1,0:T(8,128)(2,1)S(1)}, u32[]{:S(2)}, u32[]{:S(2)}) collective-permute-start(bf16[1024,128]{1,0:T(8,128)(2,1)} %copy-done.42), channel_id=1, source_target_pairs={{0,5},{1,4},{2,7},{3,6},{4,1},{5,0},{6,3},{7,2},{8,13},{9,12},{10,... | collective-permute-start | bytes 786440 | tf_op jit(solution)/shard_map/ppermute | solution.py:334
  159.6 32.6 %collective-permute-start.10 = (bf16[1024,128]{1,0:T(8,128)(2,1)S(1)}, bf16[1024,128]{1,0:T(8,128)(2,1)S(1)}, u32[]{:S(2)}, u32[]{:S(2)}) collective-permute-start(bf16[1024,128]{1,0:T(8,128)(2,1)S(1)} %copy-done.41), channel_id=1, source_target_pairs={{0,6},{1,7},{2,4},{3,5},{4,2},{5,3},{6,0},{7,1},{8,14},{9,15},{10,... | collective-permute-start | bytes 786440 | tf_op jit(solution)/shard_map/ppermute | solution.py:334
  166.8 32.9 %collective-permute-start.11 = (bf16[1024,128]{1,0:T(8,128)(2,1)S(1)}, bf16[1024,128]{1,0:T(8,128)(2,1)S(1)}, u32[]{:S(2)}, u32[]{:S(2)}) collective-permute-start(bf16[1024,128]{1,0:T(8,128)(2,1)S(1)} %copy-done.39), channel_id=1, source_target_pairs={{0,7},{1,6},{2,5},{3,4},{4,3},{5,2},{6,1},{7,0},{8,15},{9,14},{10,... | collective-permute-start | bytes 786440 | tf_op jit(solution)/shard_map/ppermute | solution.py:334
  216.9 11.8 %collective-permute-start.28 = (bf16[96,1024]{1,0:T(8,128)(2,1)S(1)}, bf16[96,1024]{1,0:T(8,128)(2,1)S(1)}, u32[]{:S(2)}, u32[]{:S(2)}) collective-permute-start(bf16[96,1024]{1,0:T(8,128)(2,1)S(1)} %get-tuple-element.94), channel_id=1, source_target_pairs={{0,2},{1,3},{2,0},{3,1},{4,6},{5,7},{6,4},{7,5},{8,10},{9,11},{10,... | collective-permute-start | bytes 589832 | tf_op jit(solution)/shard_map/ppermute | solution.py:334
  218.7 27.9 %collective-permute-start.29 = (bf16[96,1024]{1,0:T(8,128)(2,1)}, bf16[96,1024]{1,0:T(8,128)(2,1)}, u32[]{:S(2)}, u32[]{:S(2)}) collective-permute-start(bf16[96,1024]{1,0:T(8,128)(2,1)} %get-tuple-element.95), channel_id=1, source_target_pairs={{0,3},{1,2},{2,1},{3,0},{4,7},{5,6},{6,5},{7,4},{8,11},{9,10},{10,... | collective-permute-start | bytes 589832 | tf_op jit(solution)/shard_map/ppermute | solution.py:334
  221.6 25.0 %collective-permute-start.30 = (bf16[96,1024]{1,0:T(8,128)(2,1)}, bf16[96,1024]{1,0:T(8,128)(2,1)}, u32[]{:S(2)}, u32[]{:S(2)}) collective-permute-start(bf16[96,1024]{1,0:T(8,128)(2,1)} %get-tuple-element.96), channel_id=1, source_target_pairs={{0,4},{1,5},{2,6},{3,7},{4,0},{5,1},{6,2},{7,3},{8,12},{9,13},{10,... | collective-permute-start | bytes 589832 | tf_op jit(solution)/shard_map/ppermute | solution.py:334
  223.1 24.5 %collective-permute-start.31 = (bf16[96,1024]{1,0:T(8,128)(2,1)}, bf16[96,1024]{1,0:T(8,128)(2,1)}, u32[]{:S(2)}, u32[]{:S(2)}) collective-permute-start(bf16[96,1024]{1,0:T(8,128)(2,1)} %get-tuple-element.97), channel_id=1, source_target_pairs={{0,5},{1,4},{2,7},{3,6},{4,1},{5,0},{6,3},{7,2},{8,13},{9,12},{10,... | collective-permute-start | bytes 589832 | tf_op jit(solution)/shard_map/ppermute | solution.py:334
  224.7 26.6 %collective-permute-start.32 = (bf16[96,1024]{1,0:T(8,128)(2,1)}, bf16[96,1024]{1,0:T(8,128)(2,1)}, u32[]{:S(2)}, u32[]{:S(2)}) collective-permute-start(bf16[96,1024]{1,0:T(8,128)(2,1)} %get-tuple-element.98), channel_id=1, source_target_pairs={{0,6},{1,7},{2,4},{3,5},{4,2},{5,3},{6,0},{7,1},{8,14},{9,15},{10,... | collective-permute-start | bytes 589832 | tf_op jit(solution)/shard_map/ppermute | solution.py:334
  228.7 25.2 %collective-permute-start.33 = (bf16[96,1024]{1,0:T(8,128)(2,1)}, bf16[96,1024]{1,0:T(8,128)(2,1)}, u32[]{:S(2)}, u32[]{:S(2)}) collective-permute-start(bf16[96,1024]{1,0:T(8,128)(2,1)} %get-tuple-element.99), channel_id=1, source_target_pairs={{0,7},{1,6},{2,5},{3,4},{4,3},{5,2},{6,1},{7,0},{8,15},{9,14},{10,... | collective-permute-start | bytes 589832 | tf_op jit(solution)/shard_map/ppermute | solution.py:334
  246.6 11.2 %collective-permute-start.35 = (bf16[32,1024]{1,0:T(8,128)(2,1)S(1)}, bf16[32,1024]{1,0:T(8,128)(2,1)S(1)}, u32[]{:S(2)}, u32[]{:S(2)}) collective-permute-start(bf16[32,1024]{1,0:T(8,128)(2,1)S(1)} %get-tuple-element.102), channel_id=1, source_target_pairs={{0,2},{1,3},{2,0},{3,1},{4,6},{5,7},{6,4},{7,5},{8,10},{9,11},{10,... | collective-permute-start | bytes 196616 | tf_op jit(solution)/shard_map/ppermute | solution.py:334
  247.6 13.8 %collective-permute-start.36 = (bf16[32,1024]{1,0:T(8,128)(2,1)S(1)}, bf16[32,1024]{1,0:T(8,128)(2,1)S(1)}, u32[]{:S(2)}, u32[]{:S(2)}) collective-permute-start(bf16[32,1024]{1,0:T(8,128)(2,1)S(1)} %get-tuple-element.103), channel_id=1, source_target_pairs={{0,3},{1,2},{2,1},{3,0},{4,7},{5,6},{6,5},{7,4},{8,11},{9,10},{10,... | collective-permute-start | bytes 196616 | tf_op jit(solution)/shard_map/ppermute | solution.py:334
  269.1 57.4 %all-to-all-start.3 = ((bf16[32,48,128]{2,1,0:T(8,128)(2,1)}), bf16[32,48,128]{2,1,0:T(8,128)(2,1)}, u32[]{:S(2)}, u32[]{:S(2)}) async-start(bf16[32,48,128]{2,1,0:T(8,128)(2,1)} %shard_map.112), calls=%async_computation.3 | async-start | bytes 786432 | tf_op jit(solution)/shard_map/all_to_all | solution.py:494
  278.7 27.6 %collective-permute-start.20 = (bf16[1024,128]{1,0:T(8,128)(2,1)}, bf16[1024,128]{1,0:T(8,128)(2,1)S(1)}, u32[]{:S(2)}, u32[]{:S(2)}) collective-permute-start(bf16[1024,128]{1,0:T(8,128)(2,1)} %copy-done.32), channel_id=1, source_target_pairs={{0,2},{1,3},{2,0},{3,1},{4,6},{5,7},{6,4},{7,5},{8,10},{9,11},{10,... | collective-permute-start | bytes 786440 | tf_op jit(solution)/shard_map/ppermute | solution.py:334
  283.2 23.9 %collective-permute-start.21 = (bf16[1024,128]{1,0:T(8,128)(2,1)}, bf16[1024,128]{1,0:T(8,128)(2,1)}, u32[]{:S(2)}, u32[]{:S(2)}) collective-permute-start(bf16[1024,128]{1,0:T(8,128)(2,1)} %copy-done.31), channel_id=1, source_target_pairs={{0,3},{1,2},{2,1},{3,0},{4,7},{5,6},{6,5},{7,4},{8,11},{9,10},{10,... | collective-permute-start | bytes 786440 | tf_op jit(solution)/shard_map/ppermute | solution.py:334
  283.3 23.8 %collective-permute-start.22 = (bf16[1024,128]{1,0:T(8,128)(2,1)}, bf16[1024,128]{1,0:T(8,128)(2,1)}, u32[]{:S(2)}, u32[]{:S(2)}) collective-permute-start(bf16[1024,128]{1,0:T(8,128)(2,1)} %copy-done.30), channel_id=1, source_target_pairs={{0,4},{1,5},{2,6},{3,7},{4,0},{5,1},{6,2},{7,3},{8,12},{9,13},{10,... | collective-permute-start | bytes 786440 | tf_op jit(solution)/shard_map/ppermute | solution.py:334
  284.5 22.7 %collective-permute-start.23 = (bf16[1024,128]{1,0:T(8,128)(2,1)}, bf16[1024,128]{1,0:T(8,128)(2,1)}, u32[]{:S(2)}, u32[]{:S(2)}) collective-permute-start(bf16[1024,128]{1,0:T(8,128)(2,1)} %copy-done.29), channel_id=1, source_target_pairs={{0,5},{1,4},{2,7},{3,6},{4,1},{5,0},{6,3},{7,2},{8,13},{9,12},{10,... | collective-permute-start | bytes 786440 | tf_op jit(solution)/shard_map/ppermute | solution.py:334
  288.7 18.5 %collective-permute-start.24 = (bf16[1024,128]{1,0:T(8,128)(2,1)}, bf16[1024,128]{1,0:T(8,128)(2,1)}, u32[]{:S(2)}, u32[]{:S(2)}) collective-permute-start(bf16[1024,128]{1,0:T(8,128)(2,1)} %copy-done.28), channel_id=1, source_target_pairs={{0,6},{1,7},{2,4},{3,5},{4,2},{5,3},{6,0},{7,1},{8,14},{9,15},{10,... | collective-permute-start | bytes 786440 | tf_op jit(solution)/shard_map/ppermute | solution.py:334
  (60 other events, 434.6 us)
